TPU v7x, 256 devices: a whole 4x4x8 slice. The times are simulated.
256 devices in a mesh: row: 16 (over y, x_lo, core), col: 16 (over x_hi, z).
Axes of the slice: x: 4 (x_hi: 2, x_lo: 2; x = x_hi * 2 + x_lo), y: 4, z: 8, core: 2. Of those that a mesh axis runs over, the one named last changes fastest.
Arguments:
- frames: bfloat16 [2, 64, 128, 2048], P(None, None, 'row', 'col'), may hold values from -6 to 6
- state: bfloat16 [64, 128, 2048], P(None, 'row', 'col'), may hold values from -1 to 1
- input_weight: bfloat16 [9, 192, 64], replicated, may hold values from -0.25 to 0.25
- state_weight: bfloat16 [9, 192, 64], replicated, may hold values from -0.25 to 0.25
- cotangent: bfloat16 [64, 128, 2048], P(None, 'row', 'col'), may hold values from -6 to 6
Outputs:
- final_state: bfloat16 [64, 128, 2048], P(None, 'row', 'col')
- grad_state: float32 [64, 128, 2048], P(None, 'row', 'col')
- grad_input_weights: float32 [9, 192, 64], replicated
- grad_state_weights: float32 [9, 192, 64], replicated
All inputs are finite; a program needn't handle non-finite values.
Results may differ from a plain program's by a relative error of at most 0.0048.
Values may be sent and summed in bfloat16 or wider, within the bound.
A program may use at most 64 MiB of HBM per device.

v0:
```python
import functools

import jax
import jax.numpy as jnp
from jax import lax
from jax.experimental import pallas as pl
from jax.experimental.pallas import tpu as pltpu
from jax.sharding import PartitionSpec as P

HALO = 4


def padded_2(array, sides, width):
    for axis, dim in sides:
        devices, length = (lax.axis_size(axis), array.shape[dim])
        up = [(i, (i + 1) % devices) for i in range(devices - 1)]
        down = [(j, i) for i, j in up]
        last = lax.slice_in_dim(array, length - width, length, axis=dim)
        first = lax.slice_in_dim(array, 0, width, axis=dim)
        before = lax.ppermute(last, axis, up)
        after = lax.ppermute(first, axis, down)
        array = jnp.concatenate([before, array, after], axis=dim)
    return array


def shifted(flat, offsets, margin, length):
    return jnp.concatenate([flat[:, margin + off : margin + off + length] for off in offsets], 0)


def conv_flat(weights, flat, offsets, margin, length):
    taps, out_ch, in_ch = weights.shape
    stack = shifted(flat, offsets, margin, length)
    matrix = weights.transpose(1, 0, 2).reshape(out_ch, taps * in_ch)
    return jnp.dot(matrix, stack, preferred_element_type=jnp.float32)


def spread_flat(weights, flat, offsets, margin, length):
    taps, out_ch, in_ch = weights.shape
    stack = shifted(flat, [-off for off in offsets], margin, length)
    matrix = weights.transpose(2, 0, 1).reshape(in_ch, taps * out_ch)
    return jnp.dot(matrix, stack, preferred_element_type=jnp.float32)


def weight_flat(pre_grad, flat, offsets, margin, length):
    taps = len(offsets)
    stack = shifted(flat, offsets, margin, length)
    share = lax.dot_general(
        pre_grad, stack, (((1,), (1,)), ((), ())), preferred_element_type=jnp.float32
    )
    return share.reshape(pre_grad.shape[0], taps, -1).transpose(1, 0, 2)


def gates(from_input, from_state, previous, channels):
    update = jax.nn.sigmoid(from_input[:channels] + from_state[:channels])
    reset_gate = jax.nn.sigmoid(
        from_input[channels : 2 * channels] + from_state[channels : 2 * channels]
    )
    state_term = from_state[2 * channels :]
    candidate = jnp.tanh(from_input[2 * channels :] + reset_gate * state_term)
    new_state = ((1.0 - update) * candidate + update * previous.astype(jnp.float32)).astype(
        jnp.bfloat16
    )
    return new_state, (update, reset_gate, candidate, state_term)


def gate_grads(grad_state, saved, previous):
    update, reset_gate, candidate, state_term = saved
    grad_candidate = grad_state * (1.0 - update)
    grad_update = grad_state * (previous.astype(jnp.float32) - candidate)
    pre_update = grad_update * update * (1.0 - update)
    pre_candidate = grad_candidate * (1.0 - candidate * candidate)
    pre_reset = pre_candidate * state_term * reset_gate * (1.0 - reset_gate)
    pre_hidden = pre_candidate * reset_gate
    input_pre = jnp.concatenate([pre_update, pre_reset, pre_candidate], 0).astype(jnp.bfloat16)
    state_pre = jnp.concatenate([pre_update, pre_reset, pre_hidden], 0).astype(jnp.bfloat16)
    return (input_pre, state_pre, grad_state * update)


def reduce_kernel(rows, cols, x_ref, out_ref, got_row, summed, got_col, reduced, gathered, send_sem, recv_sem, own_sem):
    mesh_ids = pl.DeviceIdType.MESH
    me_row, me_col = lax.axis_index("row"), lax.axis_index("col")
    barrier = pltpu.get_barrier_semaphore()
    for axis, me, count in (("row", me_row, rows), ("col", me_col, cols)):
        for distance in range(1, count):
            peer = lax.rem(me + distance, count)
            pl.semaphore_signal(barrier, inc=1, device_id={axis: peer}, device_id_type=mesh_ids)
    pl.semaphore_wait(barrier, rows + cols - 2)
    piece = summed.shape[0] // cols

    def phase(index, axis, me, count, source, target):
        copies = []
        for distance in range(1, count):
            peer = lax.rem(me + distance, count)
            copy = pltpu.make_async_remote_copy(
                src_ref=source(peer),
                dst_ref=target.at[me],
                send_sem=send_sem.at[index, distance],
                recv_sem=recv_sem.at[index, distance],
                device_id={axis: peer},
                device_id_type=mesh_ids,
            )
            copy.start()
            copies.append(copy)
        own = pltpu.make_async_copy(source(me), target.at[me], own_sem.at[index])
        own.start()
        own.wait()
        for copy in copies:
            copy.wait()

    phase(0, "row", me_row, rows, lambda peer: x_ref.at[peer], got_row)
    total = got_row[0]
    for index in range(1, rows):
        total = total + got_row[index]
    summed[...] = total
    phase(
        1, "col", me_col, cols,
        lambda peer: summed.at[pl.ds(pl.multiple_of(peer * piece, piece), piece)], got_col,
    )
    total = got_col[0]
    for index in range(1, cols):
        total = total + got_col[index]
    reduced[...] = total
    phase(2, "col", me_col, cols, lambda peer: reduced, gathered)
    phase(3, "row", me_row, rows, lambda peer: gathered, out_ref)


def all_sum(parts):
    both = jnp.stack(parts, 0)
    rows, cols = lax.axis_size("row"), lax.axis_size("col")
    lanes = 128
    piece = -(-both.size // (rows * cols * lanes))
    piece = -(-piece // 8) * 8
    chunk = cols * piece * lanes
    padded_size = rows * chunk
    flat = jnp.pad(both.reshape(-1), (0, padded_size - both.size))
    count = max(rows, cols)
    out = pl.pallas_call(
        functools.partial(reduce_kernel, rows, cols),
        out_shape=jax.ShapeDtypeStruct((rows, cols, piece, lanes), jnp.float32),
        in_specs=[pl.BlockSpec(memory_space=pltpu.VMEM)],
        out_specs=pl.BlockSpec(memory_space=pltpu.VMEM),
        scratch_shapes=[
            pltpu.VMEM((rows, cols * piece, lanes), jnp.float32),
            pltpu.VMEM((cols * piece, lanes), jnp.float32),
            pltpu.VMEM((cols, piece, lanes), jnp.float32),
            pltpu.VMEM((piece, lanes), jnp.float32),
            pltpu.VMEM((cols, piece, lanes), jnp.float32),
            pltpu.SemaphoreType.DMA((4, count)),
            pltpu.SemaphoreType.DMA((4, count)),
            pltpu.SemaphoreType.DMA((4,)),
        ],
        compiler_params=pltpu.CompilerParams(collective_id=0, has_side_effects=True),
    )(flat.reshape(rows, cols * piece, lanes))
    return out.reshape(-1)[: both.size].reshape(both.shape)


def local(frames, state, input_weight, state_weight, cotangent):
    step_count = frames.shape[0]
    channels = state.shape[0]
    rows, cols = state.shape[1], state.shape[2]
    halo = HALO
    ext_rows, ext_cols = rows + 2 * halo, cols + 2 * halo
    length = ext_rows * ext_cols
    margin = ext_cols + 1
    offsets = [(k // 3 - 1) * ext_cols + (k % 3 - 1) for k in range(9)]

    fields = jnp.concatenate([frames.reshape(-1, rows, cols), state, cotangent], 0)
    fields = padded_2(fields, (("row", 1), ("col", 2)), halo).reshape(-1, length)
    frame_flat = [fields[t * frames.shape[1] : (t + 1) * frames.shape[1]] for t in range(step_count)]
    base = step_count * frames.shape[1]
    state_flat = fields[base : base + channels]
    cot_flat = fields[base + channels :]

    r = lax.broadcasted_iota(jnp.int32, (ext_rows, ext_cols), 0)
    c = lax.broadcasted_iota(jnp.int32, (ext_rows, ext_cols), 1)
    global_r = lax.axis_index("row") * rows + r - halo
    global_c = lax.axis_index("col") * cols + c - halo
    inside = (
        (global_r >= 0)
        & (global_r < rows * lax.axis_size("row"))
        & (global_c >= 0)
        & (global_c < cols * lax.axis_size("col"))
    ).reshape(1, length)
    own = ((r >= halo) & (r < halo + rows) & (c >= halo) & (c < halo + cols)).reshape(1, length)

    def pad(flat):
        return jnp.pad(flat, ((0, 0), (margin, margin)))

    records = []
    current = state_flat
    for step_index in range(step_count):
        frame_pad, state_pad = pad(frame_flat[step_index]), pad(current)
        from_input = conv_flat(input_weight, frame_pad, offsets, margin, length)
        from_state = conv_flat(state_weight, state_pad, offsets, margin, length)
        new_state, saved = gates(from_input, from_state, current, channels)
        records.append((frame_pad, state_pad, current, saved))
        current = jnp.where(inside, new_state, jnp.zeros_like(new_state))

    grad_state = cot_flat.astype(jnp.float32)
    input_pres, input_fields, state_pres, state_fields = [], [], [], []
    for step_index in reversed(range(step_count)):
        frame_pad, state_pad, previous, saved = records[step_index]
        input_pre, state_pre, direct = gate_grads(grad_state, saved, previous)
        input_pres.append(jnp.where(own, input_pre, jnp.zeros_like(input_pre)))
        state_pres.append(jnp.where(own, state_pre, jnp.zeros_like(state_pre)))
        input_fields.append(frame_pad)
        state_fields.append(state_pad)
        state_pre = jnp.where(inside, state_pre, jnp.zeros_like(state_pre))
        grad_state = direct + spread_flat(state_weight, pad(state_pre), offsets, margin, length)

    input_sum = sum(
        weight_flat(p, f, offsets, margin, length) for p, f in zip(input_pres, input_fields)
    )
    state_sum = sum(
        weight_flat(p, f, offsets, margin, length) for p, f in zip(state_pres, state_fields)
    )
    input_sum, state_sum = all_sum([input_sum, state_sum])
    loss_scale = (rows * lax.axis_size("row") * cols * lax.axis_size("col")) ** (-0.5)

    def crop(flat):
        return flat.reshape(-1, ext_rows, ext_cols)[:, halo : halo + rows, halo : halo + cols]

    return (crop(current), crop(grad_state), input_sum * loss_scale, state_sum * loss_scale)


def solution(mesh):
    in_specs = (P(None, None, "row", "col"), P(None, "row", "col"), P(), P(), P(None, "row", "col"))
    out_specs = (P(None, "row", "col"), P(None, "row", "col"), P(), P())
    return jax.shard_map(local, mesh=mesh, in_specs=in_specs, out_specs=out_specs, check_vma=False)
```

profile of v0, /device:TPU:1, one launch (start us, length us, event | category | flops | bytes accessed | tf_op | source)
XLA Modules:
  0.0 149.7 jit_solution(3975130016069637597)
XLA Ops:
  0.6 1.2 pad_maximum_fusion.9
  2.0 4.5 %collective-permute-start = (bf16[256,4,128]{2,1,0:T(4,128)(2,1)S(1)}, bf16[256,4,128]{2,1,0:T(4,128)(2,1)S(1)}, u32[]{:S(2)}, u32[]{:S(2)}) collective-permute-start(bf16[256,4,128]{2,1,0:T(4,128)(2,1)S(1)} %get-tuple-element.38), channel_id=1, source_target_pairs={{0,16},{16,32},{32,48},{48,64},{64,80},{80,96},{96,112},{112,128},... | collective-permute-start | bytes 786440 | tf_op jit(solution)/shard_map/ppermute | solution.py:20
  6.5 1.9 %collective-permute-start.1 = (bf16[256,4,128]{2,1,0:T(4,128)(2,1)S(1)}, bf16[256,4,128]{2,1,0:T(4,128)(2,1)S(1)}, u32[]{:S(2)}, u32[]{:S(2)}) collective-permute-start(bf16[256,4,128]{2,1,0:T(4,128)(2,1)S(1)} %get-tuple-element.39), channel_id=1, source_target_pairs={{16,0},{32,16},{48,32},{64,48},{80,64},{96,80},{112,96},{128,112},... | collective-permute-start | bytes 786440 | tf_op jit(solution)/shard_map/ppermute | solution.py:21
  8.6 1.2 collective-permute-done
  9.8 4.5 %collective-permute-done.1 = bf16[256,4,128]{2,1,0:T(4,128)(2,1)S(1)} collective-permute-done((bf16[256,4,128]{2,1,0:T(4,128)(2,1)S(1)}, bf16[256,4,128]{2,1,0:T(4,128)(2,1)S(1)}, u32[]{:S(2)}, u32[]{:S(2)}) %collective-permute-start.1) | collective-permute-done | bytes 262176 | tf_op jit(solution)/shard_map/ppermute | solution.py:21
  14.3 0.7 copy-done.25
  15.1 1.7 %pad_maximum_fusion.2 = bf16[256,16,128]{2,1,0:T(8,128)(2,1)S(1)} fusion(bf16[256,4,128]{2,1,0:T(4,128)(2,1)S(1)} %collective-permute-done.1, bf16[64,8,128]{2,1,0:T(8,128)(2,1)} %param.9, bf16[64,8,128]{2,1,0:T(8,128)(2,1)} %param.6, bf16[128,8,128]{2,1,0:T(8,128)(2,1)} %bitcast.64, bf16[256,4,128]{2,1,0:T(4,128)(2,1)S(1)} %collective-permute-done), kind=kLoop, calls=%fused_computation.12 | loop fusion | flops 5242880 | bytes 2097152 | tf_op jit(solution)/shard_map/concatenate | solution.py:22
  17.2 0.9 copy.26
  18.2 0.9 copy.27
  19.1 1.3 collective-permute-start.3
  20.4 4.2 %collective-permute-start.2 = (bf16[256,16,4]{0,1,2:T(8,128)(2,1)S(1)}, bf16[256,16,4]{0,1,2:T(8,128)(2,1)S(1)}, u32[]{:S(2)}, u32[]{:S(2)}) collective-permute-start(bf16[256,16,4]{0,1,2:T(8,128)(2,1)S(1)} %copy.26), channel_id=1, source_target_pairs={{0,1},{1,2},{2,3},{3,4},{4,5},{5,6},{6,7},{7,8},{8,9},{9,10},{10,1... | collective-permute-start | bytes 98312 | tf_op jit(solution)/shard_map/ppermute | solution.py:20
  24.6 0.7 and.82
  25.4 0.7 and.78
  26.6 1.0 copy.28
  27.7 1.0 copy.29
  28.7 6.2 %pad_maximum_fusion = bf16[256,16,136]{2,1,0:T(8,128)(2,1)S(1)} fusion(bf16[256,16,4]{2,1,0:T(8,128)(2,1)S(1)} %copy.29, bf16[256,4,128]{2,1,0:T(4,128)(2,1)} %copy-done.25, bf16[64,8,128]{2,1,0:T(8,128)(2,1)S(1)} %copy-done.20, bf16[64,8,128]{2,1,0:T(8,128)(2,1)S(1)} %copy-done.21, bf16[128,8,128]{2,1,0:T(8,128)(2,1)S(1)} %bitcast.65, ...), kind=kLoop, calls=%fused_computation.8 | loop fusion | flops 7798784 | bytes 2228224 | tf_op jit(solution)/shard_map/concatenate | solution.py:22
  34.9 1.0 fusion.64
  35.9 1.7 %slice.276 = bf16[64,2176]{1,0:T(8,128)(2,1)S(1)} reshape(bf16[64,16,136]{2,1,0:T(8,128)(2,1)} %get-tuple-element.29) | data formatting | bytes 557056 | tf_op jit(solution)/shard_map/slice | solution.py:169
  37.7 0.7 slice.298
  38.3 0.7 slice.287
  39.0 1.4 reshape.139
  43.0 0.9 convolution_bitcast_fusion.2
  44.3 0.9 convolution_bitcast_fusion.1
  45.2 1.4 fusion.47
  47.8 0.9 convolution_bitcast_fusion
  50.0 0.9 convolution_bitcast_fusion.3
  51.6 0.9 fusion.46
  53.1 2.0 %fusion.6 = f32[192,576]{1,0:T(8,128)} fusion(bf16[576,2176]{1,0:T(8,128)(2,1)S(1)} %slice_dynamic-update-slice_fusion.16, pred[2176]{0:T(1024)(128)(4,1)S(1)} %copy-done.27, bf16[64,2176]{1,0:T(8,128)(2,1)S(1)} %get-tuple-element.28, bf16[64,2176]{1,0:T(8,128)(2,1)S(1)} %get-tuple-element.27, bf16[64,2176]{1,0:T(8,128)(2,1)S(1)} %fusion.23), kind=kOutput, calls=%fused_computation.23 | convolution fusion | flops 484220928 | bytes 3786880 | tf_op jit(solution)/shard_map/dot_general | solution.py:47
  55.1 1.9 %fusion.2 = f32[192,576]{1,0:T(8,128)} fusion(bf16[576,2176]{1,0:T(8,128)(2,1)S(1)} %slice_dynamic-update-slice_fusion.40, bf16[64,2176]{1,0:T(8,128)(2,1)S(1)} %get-tuple-element.18, pred[2176]{0:T(1024)(128)(4,1)S(1)} %copy-done.27, bf16[64,2176]{1,0:T(8,128)(2,1)S(1)} %get-tuple-element.27, bf16[64,2176]{1,0:T(8,128)(2,1)S(1)} %fusion.23), kind=kOutput, calls=%fused_computation.18 | convolution fusion | flops 484220928 | bytes 3786880 | tf_op jit(solution)/shard_map/dot_general | solution.py:47
  57.0 3.2 %reshape.133 = bf16[64,16,136]{2,1,0:T(8,128)(2,1)} reshape(bf16[64,2176]{1,0:T(8,128)(2,1)} %fusion.46) | data formatting | bytes 557056 | tf_op jit(solution)/shard_map/reshape | solution.py:221
  60.2 1.8 %slice.363 = bf16[64,8,128]{2,1,0:T(8,128)(2,1)} slice(bf16[64,16,136]{2,1,0:T(8,128)(2,1)} %reshape.133), slice={[0:64], [4:12], [4:132]} | slice | bytes 262144 | tf_op jit(solution)/shard_map/slice | solution.py:221
  65.3 2.5 %fusion.58 = (bf16[64,2176]{1,0:T(8,128)(2,1)}, f32[64,2176]{1,0:T(8,128)S(1)}, bf16[64,2176]{1,0:T(8,128)(2,1)S(1)}, f32[64,2176]{1,0:T(8,128)}) fusion(f32[64,2176]{1,0:T(8,128)S(1)} %copy-done.18, f32[64,2176]{1,0:T(8,128)S(1)} %copy-done.11, bf16[64,2176]{1,0:T(8,128)(2,1)S(1)} %slice.298, bf16[64,1728]{1,0:T(8,128)(2,1)S(1)} %reshape.134, ...), kind=kOutput, calls=%fused_computation.158 | convolution fusion | flops 483246080 | bytes 11919360 | tf_op jit(solution)/shard_map/dot_general | solution.py:41
  67.8 1.5 multiply_convert_fusion.1
  69.5 0.5 copy-done.23
  70.0 1.8 %convolution_add_fusion = f32[192,576]{1,0:T(8,128)} fusion(f32[192,576]{1,0:T(8,128)S(1)} %copy-done.28, bf16[576,2176]{1,0:T(8,128)(2,1)S(1)} %copy-done.10, pred[2176]{0:T(1024)(128)(4,1)S(1)} %copy-done.27, bf16[64,2176]{1,0:T(8,128)(2,1)S(1)} %get-tuple-element.26, bf16[64,2176]{1,0:T(8,128)(2,1)S(1)} %get-tuple-element.25, ...), kind=kOutput, calls=%fused_computation.9 | convolution fusion | flops 484331520 | bytes 4229248 | tf_op jit(solution)/shard_map/dot_general | solution.py:47
  71.9 2.1 %copy.32 = f32[192,576]{0,1:T(8,128)} copy(f32[192,576]{1,0:T(8,128)} %convolution_add_fusion) | data formatting | bytes 884736 | tf_op jit(solution)/shard_map/add | solution.py:214
  73.9 3.1 %convolution_add_fusion.1 = f32[192,576]{1,0:T(8,128)} fusion(f32[192,576]{1,0:T(8,128)} %fusion.2, bf16[576,2176]{1,0:T(8,128)(2,1)S(1)} %copy-done.8, bf16[64,2176]{1,0:T(8,128)(2,1)} %get-tuple-element.16, pred[2176]{0:T(1024)(128)(4,1)S(1)} %copy-done.27, bf16[64,2176]{1,0:T(8,128)(2,1)} %copy-done.23, bf16[64,2176]{1,0:T(8,128)(2,1)} %copy-done.22), kind=kOutput, calls=%fused_computation.10 | convolution fusion | flops 484331520 | bytes 4229248 | tf_op jit(solution)/shard_map/dot_general | solution.py:47
  77.0 1.2 copy.31
  78.3 2.2 %pad_maximum_fusion.1 = f32[2,9,192,64]{2,3,1,0:T(8,128)} fusion(f32[1,9,192,64]{2,3,1,0:T(8,128)} %bitcast.61, f32[1,9,192,64]{2,3,1,0:T(8,128)S(1)} %bitcast.62), kind=kLoop, calls=%fused_computation.11 | loop fusion | flops 221184 | bytes 1769472 | tf_op jit(solution)/shard_map/stack | solution.py:128
  80.5 1.8 %copy.33 = f32[2,9,192,64]{3,2,1,0:T(8,128)S(1)} copy(f32[2,9,192,64]{2,3,1,0:T(8,128)} %pad_maximum_fusion.1) | data formatting | bytes 1769472 | tf_op jit(solution)/shard_map/stack | solution.py:128
  82.6 1.1 pad.30
  83.6 55.5 %shard_map.84 = f32[16,16,8,128]{3,2,1,0:T(8,128)} custom-call(f32[16,128,128]{2,1,0:T(8,128)} %bitcast.56), custom_call_target="tpu_custom_call" | custom-call | tf_op jit(solution)/shard_map/pallas_call | solution.py:137
  139.1 1.2 slice_multiply_fusion
  140.6 1.2 copy.35
  141.9 1.2 copy.34
  146.1 1.4 fusion
  147.5 1.4 reshape.135
  148.9 0.8 slice.365
  (130 shorter events, 15.0 us)
Async XLA Ops:
  0.6 42.2 %copy-start = (bf16[9,192,64]{1,2,0:T(8,128)(2,1)S(1)}, bf16[9,192,64]{1,2,0:T(8,128)(2,1)}, u32[]{:S(2)}) copy-start(bf16[9,192,64]{1,2,0:T(8,128)(2,1)} %param.7) | copy-start | bytes 663556
  2.0 7.8 %collective-permute-start = (bf16[256,4,128]{2,1,0:T(4,128)(2,1)S(1)}, bf16[256,4,128]{2,1,0:T(4,128)(2,1)S(1)}, u32[]{:S(2)}, u32[]{:S(2)}) collective-permute-start(bf16[256,4,128]{2,1,0:T(4,128)(2,1)S(1)} %get-tuple-element.38), channel_id=1, source_target_pairs={{0,16},{16,32},{32,48},{48,64},{64,80},{80,96},{96,112},{112,128},... | collective-permute-start | bytes 786440 | tf_op jit(solution)/shard_map/ppermute | solution.py:20
  6.5 7.8 %collective-permute-start.1 = (bf16[256,4,128]{2,1,0:T(4,128)(2,1)S(1)}, bf16[256,4,128]{2,1,0:T(4,128)(2,1)S(1)}, u32[]{:S(2)}, u32[]{:S(2)}) collective-permute-start(bf16[256,4,128]{2,1,0:T(4,128)(2,1)S(1)} %get-tuple-element.39), channel_id=1, source_target_pairs={{16,0},{32,16},{48,32},{64,48},{80,64},{96,80},{112,96},{128,112},... | collective-permute-start | bytes 786440 | tf_op jit(solution)/shard_map/ppermute | solution.py:21
  9.8 4.5 %copy-start.24 = (bf16[256,4,128]{2,1,0:T(4,128)(2,1)}, bf16[256,4,128]{2,1,0:T(4,128)(2,1)S(1)}, u32[]{:S(2)}) copy-start(bf16[256,4,128]{2,1,0:T(4,128)(2,1)S(1)} %collective-permute-done) | copy-start | bytes 786436
  14.3 0.7 copy-start.25
  16.7 9.3 %copy-start.15 = (bf16[9,192,64]{1,2,0:T(8,128)(2,1)S(1)}, bf16[9,192,64]{1,2,0:T(8,128)(2,1)}, u32[]{:S(2)}) copy-start(bf16[9,192,64]{1,2,0:T(8,128)(2,1)} %param.8) | copy-start | bytes 663556
  18.1 10.5 %copy-start.17 = (bf16[2,64,8,128]{3,2,1,0:T(8,128)(2,1)S(1)}, bf16[2,64,8,128]{3,2,1,0:T(8,128)(2,1)}, u32[]{:S(2)}) copy-start(bf16[2,64,8,128]{3,2,1,0:T(8,128)(2,1)} %param.5) | copy-start | bytes 786436
  18.1 10.5 %copy-start.20 = (bf16[64,8,128]{2,1,0:T(8,128)(2,1)S(1)}, bf16[64,8,128]{2,1,0:T(8,128)(2,1)}, u32[]{:S(2)}) copy-start(bf16[64,8,128]{2,1,0:T(8,128)(2,1)} %param.9) | copy-start | bytes 393220
  18.2 10.5 %copy-start.21 = (bf16[64,8,128]{2,1,0:T(8,128)(2,1)S(1)}, bf16[64,8,128]{2,1,0:T(8,128)(2,1)}, u32[]{:S(2)}) copy-start(bf16[64,8,128]{2,1,0:T(8,128)(2,1)} %param.6) | copy-start | bytes 393220
  19.1 8.5 %collective-permute-start.3 = (bf16[256,16,4]{0,1,2:T(8,128)(2,1)S(1)}, bf16[256,16,4]{0,1,2:T(8,128)(2,1)S(1)}, u32[]{:S(2)}, u32[]{:S(2)}) collective-permute-start(bf16[256,16,4]{0,1,2:T(8,128)(2,1)S(1)} %copy.27), channel_id=1, source_target_pairs={{1,0},{2,1},{3,2},{4,3},{5,4},{6,5},{7,6},{8,7},{9,8},{10,9},{11,1... | collective-permute-start | bytes 98312 | tf_op jit(solution)/shard_map/ppermute | solution.py:21
  20.4 6.2 %collective-permute-start.2 = (bf16[256,16,4]{0,1,2:T(8,128)(2,1)S(1)}, bf16[256,16,4]{0,1,2:T(8,128)(2,1)S(1)}, u32[]{:S(2)}, u32[]{:S(2)}) collective-permute-start(bf16[256,16,4]{0,1,2:T(8,128)(2,1)S(1)} %copy.26), channel_id=1, source_target_pairs={{0,1},{1,2},{2,3},{3,4},{4,5},{5,6},{6,7},{7,8},{8,9},{9,10},{10,1... | collective-permute-start | bytes 98312 | tf_op jit(solution)/shard_map/ppermute | solution.py:20
  26.6 38.1 %copy-start.13 = (bf16[64,1728]{1,0:T(8,128)(2,1)}, bf16[64,1728]{1,0:T(8,128)(2,1)S(1)}, u32[]{:S(2)}) copy-start(bf16[64,1728]{1,0:T(8,128)(2,1)S(1)} %reshape.134) | copy-start | bytes 663556
  41.6 1.5 copy-start.7
  42.8 1.5 %copy-start.9 = (bf16[576,2176]{1,0:T(8,128)(2,1)}, bf16[576,2176]{1,0:T(8,128)(2,1)S(1)}, u32[]{:S(2)}) copy-start(bf16[576,2176]{1,0:T(8,128)(2,1)S(1)} %slice_dynamic-update-slice_fusion.24) | copy-start | bytes 7520260
  43.0 1.3 copy-start.16
  43.9 1.3 copy-start.2
  44.3 0.9 copy-start.26
  49.9 1.1 copy-start.3
  51.4 1.3 copy-start.5
  52.4 0.7 copy-start.27
  63.7 1.1 copy-start.4
  63.8 1.2 copy-start.6
  63.8 1.4 copy-start.11
  63.8 1.5 %copy-start.18 = (f32[64,2176]{1,0:T(8,128)S(1)}, f32[64,2176]{1,0:T(8,128)}, u32[]{:S(2)}) copy-start(f32[64,2176]{1,0:T(8,128)} %get-tuple-element.23) | copy-start | bytes 1671172
  67.8 1.6 %copy-start.22 = (bf16[64,2176]{1,0:T(8,128)(2,1)}, bf16[64,2176]{1,0:T(8,128)(2,1)S(1)}, u32[]{:S(2)}) copy-start(bf16[64,2176]{1,0:T(8,128)(2,1)S(1)} %get-tuple-element.33) | copy-start | bytes 835588
  67.8 2.2 %copy-start.10 = (bf16[576,2176]{1,0:T(8,128)(2,1)S(1)}, bf16[576,2176]{1,0:T(8,128)(2,1)}, u32[]{:S(2)}) copy-start(bf16[576,2176]{1,0:T(8,128)(2,1)} %copy-done.9) | copy-start | bytes 7520260
  67.8 2.2 %copy-start.28 = (f32[192,576]{1,0:T(8,128)S(1)}, f32[192,576]{1,0:T(8,128)}, u32[]{:S(2)}) copy-start(f32[192,576]{1,0:T(8,128)} %fusion.6) | copy-start | bytes 1327108
  69.3 0.7 copy-start.23
  70.0 3.9 %copy-start.8 = (bf16[576,2176]{1,0:T(8,128)(2,1)S(1)}, bf16[576,2176]{1,0:T(8,128)(2,1)}, u32[]{:S(2)}) copy-start(bf16[576,2176]{1,0:T(8,128)(2,1)} %copy-done.7) | copy-start | bytes 7520260
  144.8 1.1 copy-start.12
  144.8 1.1 copy-start.14
  144.8 1.3 copy-start.19
  146.1 3.7 %copy-start.1 = (bf16[9,192,64]{1,2,0:T(8,128)(2,1)S(1)}, bf16[9,192,64]{1,2,0:T(8,128)(2,1)}, u32[]{:S(2)}) copy-start(bf16[9,192,64]{1,2,0:T(8,128)(2,1)} %param.7) | copy-start | bytes 663556
where the time goes:
time: 151 us; the launch traced here: 150 us
  Pallas kernels  55.5 us (37%)
  local copies, waits for them, and re-layouts  40.4 us (27%)
  other arithmetic  18.5 us (12%)
  matrix products  16.3 us (11%)
  starting transfers between devices  11.9 us (8%)
  waiting for transfers between devices  5.72 us (4%)
    pallas_call x1, Pallas kernels, all_sum(): pl.pallas_call(functools.partial(reduce_kernel, rows, cols), out_shape=ja...  55.5 us
    unnamed x108, local copies, waits for them, and re-layouts  14.2 us
    dot_general x4, matrix products, weight_flat(): lax.dot_general(pre_grad, stack, (((1,), (1,)), ((), ())), preferred_elem...  8.85 us
    ppermute x2, starting transfers between devices, padded_2(): before = lax.ppermute(last, axis, up)  8.68 us
    concatenate x2, other arithmetic, padded_2(): array = jnp.concatenate([before, array, after], axis=dim)  7.86 us
    reshape x2, local copies, waits for them, and re-layouts, crop(): flat.reshape(-1, ext_rows, ext_cols)[:, halo:halo + rows, halo:halo + cols]  4.57 us
    ppermute x2, waiting for transfers between devices, padded_2(): after = lax.ppermute(first, axis, down)  4.52 us
    dot_general x2, matrix products, spread_flat(): return jnp.dot(matrix, stack, preferred_element_type=jnp.float32)  3.96 us
  transfers between devices with their start and end apart: 4, of which 2 were waited for; matrix products, arithmetic and copies ran while one was open for 2% of the time, Pallas kernels for 0%

commit v1 on v0

--- a/solution.py
+++ b/solution.py
@@ -10,17 +10,30 @@
 HALO = 4
 
 
-def padded_2(array, sides, width):
-    for axis, dim in sides:
-        devices, length = (lax.axis_size(axis), array.shape[dim])
-        up = [(i, (i + 1) % devices) for i in range(devices - 1)]
-        down = [(j, i) for i, j in up]
-        last = lax.slice_in_dim(array, length - width, length, axis=dim)
-        first = lax.slice_in_dim(array, 0, width, axis=dim)
-        before = lax.ppermute(last, axis, up)
-        after = lax.ppermute(first, axis, down)
-        array = jnp.concatenate([before, array, after], axis=dim)
-    return array
+def halo_all(array, width):
+    rows, cols = lax.axis_size("row"), lax.axis_size("col")
+    height, breadth = array.shape[1], array.shape[2]
+    low_r, high_r = slice(0, width), slice(height - width, height)
+    low_c, high_c = slice(0, width), slice(breadth - width, breadth)
+    whole_r, whole_c = slice(0, height), slice(0, breadth)
+
+    def fetch(down, right, rows_taken, cols_taken):
+        pairs = [
+            (r * cols + c, (r + down) * cols + c + right)
+            for r in range(rows)
+            for c in range(cols)
+            if 0 <= r + down < rows and 0 <= c + right < cols
+        ]
+        return lax.ppermute(array[:, rows_taken, cols_taken], ("row", "col"), pairs)
+
+    top = jnp.concatenate(
+        [fetch(1, 1, high_r, high_c), fetch(1, 0, high_r, whole_c), fetch(1, -1, high_r, low_c)], 2
+    )
+    middle = jnp.concatenate([fetch(0, 1, whole_r, high_c), array, fetch(0, -1, whole_r, low_c)], 2)
+    bottom = jnp.concatenate(
+        [fetch(-1, 1, low_r, high_c), fetch(-1, 0, low_r, whole_c), fetch(-1, -1, low_r, low_c)], 2
+    )
+    return jnp.concatenate([top, middle, bottom], 1)
 
 
 def shifted(flat, offsets, margin, length):
@@ -165,7 +178,7 @@
     offsets = [(k // 3 - 1) * ext_cols + (k % 3 - 1) for k in range(9)]
 
     fields = jnp.concatenate([frames.reshape(-1, rows, cols), state, cotangent], 0)
-    fields = padded_2(fields, (("row", 1), ("col", 2)), halo).reshape(-1, length)
+    fields = halo_all(fields, halo).reshape(-1, length)
     frame_flat = [fields[t * frames.shape[1] : (t + 1) * frames.shape[1]] for t in range(step_count)]
     base = step_count * frames.shape[1]
     state_flat = fields[base : base + channels]

time: 151 us -> 171 us (1.13)
  starting transfers between devices: 11.9 us -> 24.8 us
  waiting for transfers between devices: 5.72 us -> 12.4 us
  Pallas kernels: 55.5 us -> 57.7 us
  local copies, waits for them, and re-layouts: 40.4 us -> 38.3 us
    ppermute x4 -> x8, starting transfers between devices: 11.9 us -> 24.8 us  [fetch(): return lax.ppermute(array[:, rows_taken, cols_taken], ('row', 'col'), pairs)]
    ppermute x4 -> x8, waiting for transfers between devices: 5.72 us -> 12.4 us  [fetch(): return lax.ppermute(array[:, rows_taken, cols_taken], ('row', 'col'), pairs)]
    pallas_call x1, Pallas kernels: 55.5 us -> 57.7 us  [all_sum(): pl.pallas_call(functools.partial(reduce_kernel, rows, cols), out_shape=ja...]
    ppermute x2 -> x0, local copies, waits for them, and re-layouts: 2.03 us -> none  [the longest x1 1.02 us: padded_2(): before = lax.ppermute(last, axis, up)]
    concatenate x2 -> x1, other arithmetic: 7.86 us -> 8.57 us  [halo_all(): return jnp.concatenate([top, middle, bottom], 1)]
    unnamed x108 -> x110, local copies, waits for them, and re-layouts: 14.2 us -> 13.5 us
  transfers between devices with their start and end apart: 4 -> 8, of which waited for: 2 -> 5; matrix products, arithmetic and copies ran while one was open for 2% -> 3% of each run, Pallas kernels for 0% -> 0%
where the time goes in v1:
time: 171 us; the launch traced here: 170 us
  Pallas kernels  57.7 us (34%)
  local copies, waits for them, and re-layouts  38.3 us (22%)
  starting transfers between devices  24.8 us (15%)
  other arithmetic  19.2 us (11%)
  matrix products  16.4 us (10%)
  waiting for transfers between devices  12.4 us (7%)
    pallas_call x1, Pallas kernels, all_sum(): pl.pallas_call(functools.partial(reduce_kernel, rows, cols), out_shape=ja...  57.7 us
    ppermute x8, starting transfers between devices, fetch(): return lax.ppermute(array[:, rows_taken, cols_taken], ('row', 'col'), pairs)  24.8 us
    unnamed x110, local copies, waits for them, and re-layouts  13.5 us
    ppermute x8, waiting for transfers between devices, fetch(): return lax.ppermute(array[:, rows_taken, cols_taken], ('row', 'col'), pairs)  12.4 us
    dot_general x4, matrix products, weight_flat(): lax.dot_general(pre_grad, stack, (((1,), (1,)), ((), ())), preferred_elem...  8.88 us
    concatenate x1, other arithmetic, halo_all(): return jnp.concatenate([top, middle, bottom], 1)  8.57 us
    reshape x2, local copies, waits for them, and re-layouts, crop(): flat.reshape(-1, ext_rows, ext_cols)[:, halo:halo + rows, halo:halo + cols]  4.57 us
    dot_general x2, matrix products, spread_flat(): return jnp.dot(matrix, stack, preferred_element_type=jnp.float32)  3.97 us
  transfers between devices with their start and end apart: 8, of which 5 were waited for; matrix products, arithmetic and copies ran while one was open for 3% of the time, Pallas kernels for 0%

profile of v1, /device:TPU:1, one launch (start us, length us, event | category | flops | bytes accessed | tf_op | source)
XLA Modules:
  0.0 170.2 jit_solution(9956795851159418007)
XLA Ops:
  0.6 1.2 pad_maximum_fusion.7
  1.8 1.0 fusion.66
  2.8 4.5 %collective-permute-start.1 = (bf16[256,4,128]{2,1,0:T(4,128)(2,1)}, bf16[256,4,128]{2,1,0:T(4,128)(2,1)}, u32[]{:S(2)}, u32[]{:S(2)}) collective-permute-start(bf16[256,4,128]{2,1,0:T(4,128)(2,1)} %get-tuple-element.32), channel_id=1, source_target_pairs={{0,16},{1,17},{2,18},{3,19},{4,20},{5,21},{6,22},{7,23},{8,24},{9,... | collective-permute-start | bytes 786440 | tf_op jit(solution)/shard_map/ppermute | solution.py:27
  7.4 2.8 %collective-permute-start.6 = (bf16[256,4,128]{2,1,0:T(4,128)(2,1)}, bf16[256,4,128]{2,1,0:T(4,128)(2,1)}, u32[]{:S(2)}, u32[]{:S(2)}) collective-permute-start(bf16[256,4,128]{2,1,0:T(4,128)(2,1)} %get-tuple-element.33), channel_id=1, source_target_pairs={{16,0},{17,1},{18,2},{19,3},{20,4},{21,5},{22,6},{23,7},{24,8},{25... | collective-permute-start | bytes 786440 | tf_op jit(solution)/shard_map/ppermute | solution.py:27
  10.1 1.2 fusion.65
  11.3 4.3 %collective-permute-start = (bf16[256,4,4]{2,1,0:T(4,128)(2,1)S(1)}, bf16[256,4,4]{2,1,0:T(4,128)(2,1)S(1)}, u32[]{:S(2)}, u32[]{:S(2)}) collective-permute-start(bf16[256,4,4]{2,1,0:T(4,128)(2,1)S(1)} %get-tuple-element.28), channel_id=1, source_target_pairs={{0,17},{1,18},{2,19},{3,20},{4,21},{5,22},{6,23},{7,24},{8,25},{9,... | collective-permute-start | bytes 24584 | tf_op jit(solution)/shard_map/ppermute | solution.py:27
  15.6 2.4 %collective-permute-start.5 = (bf16[256,4,4]{2,1,0:T(4,128)(2,1)S(1)}, bf16[256,4,4]{2,1,0:T(4,128)(2,1)S(1)}, u32[]{:S(2)}, u32[]{:S(2)}) collective-permute-start(bf16[256,4,4]{2,1,0:T(4,128)(2,1)S(1)} %get-tuple-element.29), channel_id=1, source_target_pairs={{16,1},{17,2},{18,3},{19,4},{20,5},{21,6},{22,7},{23,8},{24,9},{25... | collective-permute-start | bytes 24584 | tf_op jit(solution)/shard_map/ppermute | solution.py:27
  18.0 1.3 collective-permute-start.7
  19.3 1.0 fusion.67
  20.8 1.3 collective-permute-start.2
  22.1 1.5 collective-permute-done.5
  23.6 7.0 %collective-permute-start.3 = (bf16[256,8,4]{2,1,0:T(8,128)(2,1)}, bf16[256,8,4]{2,1,0:T(8,128)(2,1)S(1)}, u32[]{:S(2)}, u32[]{:S(2)}) collective-permute-start(bf16[256,8,4]{2,1,0:T(8,128)(2,1)} %get-tuple-element.34), channel_id=1, source_target_pairs={{0,1},{1,2},{2,3},{3,4},{4,5},{5,6},{6,7},{7,8},{8,9},{9,10},{10,1... | collective-permute-start | bytes 49160 | tf_op jit(solution)/shard_map/ppermute | solution.py:27
  30.9 1.3 collective-permute-start.4
  32.3 0.7 and.82
  33.0 0.7 and.78
  34.3 6.3 %collective-permute-done.3 = bf16[256,8,4]{2,1,0:T(8,128)(2,1)S(1)} collective-permute-done((bf16[256,8,4]{2,1,0:T(8,128)(2,1)}, bf16[256,8,4]{2,1,0:T(8,128)(2,1)S(1)}, u32[]{:S(2)}, u32[]{:S(2)}) %collective-permute-start.3) | collective-permute-done | bytes 16416 | tf_op jit(solution)/shard_map/ppermute | solution.py:27
  40.6 3.8 %collective-permute-done.4 = bf16[256,8,4]{2,1,0:T(8,128)(2,1)S(1)} collective-permute-done((bf16[256,8,4]{2,1,0:T(8,128)(2,1)S(1)}, bf16[256,8,4]{2,1,0:T(8,128)(2,1)S(1)}, u32[]{:S(2)}, u32[]{:S(2)}) %collective-permute-start.4) | collective-permute-done | bytes 16416 | tf_op jit(solution)/shard_map/ppermute | solution.py:27
  44.5 8.6 %maximum_maximum_fusion = bf16[256,16,136]{2,1,0:T(8,128)(2,1)S(1)} fusion(bf16[256,4,4]{2,1,0:T(4,128)(2,1)} %copy-done.26, bf16[256,4,128]{2,1,0:T(4,128)(2,1)} %collective-permute-done.6, bf16[256,4,4]{2,1,0:T(4,128)(2,1)} %copy-done.25, bf16[256,8,4]{2,1,0:T(8,128)(2,1)S(1)} %collective-permute-done.4, bf16[64,8,128]{2,1,0:T(8,128)(2,1)S(1)} %copy-done.22, ...), kind=kLoop, calls=%fused_computation.8 | loop fusion | flops 12255232 | bytes 2228224 | tf_op jit(solution)/shard_map/concatenate | solution.py:36
  53.1 1.0 fusion.64
  54.1 1.7 %slice.292 = bf16[64,2176]{1,0:T(8,128)(2,1)S(1)} reshape(bf16[64,16,136]{2,1,0:T(8,128)(2,1)} %get-tuple-element.21) | data formatting | bytes 557056 | tf_op jit(solution)/shard_map/slice | solution.py:182
  56.5 0.7 slice.303
  57.2 1.4 reshape.139
  61.2 0.9 convolution_bitcast_fusion.2
  62.5 0.9 convolution_bitcast_fusion.1
  63.4 1.4 fusion.47
  66.0 0.9 convolution_bitcast_fusion
  68.2 0.9 convolution_bitcast_fusion.3
  69.8 0.8 fusion.46
  71.3 2.1 %fusion.6 = f32[192,576]{1,0:T(8,128)} fusion(bf16[576,2176]{1,0:T(8,128)(2,1)S(1)} %slice_dynamic-update-slice_fusion.16, pred[2176]{0:T(1024)(128)(4,1)S(1)} %copy-done.28, bf16[64,2176]{1,0:T(8,128)(2,1)S(1)} %get-tuple-element.20, bf16[64,2176]{1,0:T(8,128)(2,1)S(1)} %get-tuple-element.19, bf16[64,2176]{1,0:T(8,128)(2,1)S(1)} %fusion.23), kind=kOutput, calls=%fused_computation.22 | convolution fusion | flops 484220928 | bytes 3786880 | tf_op jit(solution)/shard_map/dot_general | solution.py:60
  73.3 1.9 %fusion.2 = f32[192,576]{1,0:T(8,128)} fusion(bf16[576,2176]{1,0:T(8,128)(2,1)S(1)} %slice_dynamic-update-slice_fusion.40, bf16[64,2176]{1,0:T(8,128)(2,1)S(1)} %get-tuple-element.10, pred[2176]{0:T(1024)(128)(4,1)S(1)} %copy-done.28, bf16[64,2176]{1,0:T(8,128)(2,1)S(1)} %get-tuple-element.19, bf16[64,2176]{1,0:T(8,128)(2,1)S(1)} %fusion.23), kind=kOutput, calls=%fused_computation.17 | convolution fusion | flops 484220928 | bytes 3786880 | tf_op jit(solution)/shard_map/dot_general | solution.py:60
  75.2 3.2 %reshape.133 = bf16[64,16,136]{2,1,0:T(8,128)(2,1)} reshape(bf16[64,2176]{1,0:T(8,128)(2,1)} %fusion.46) | data formatting | bytes 557056 | tf_op jit(solution)/shard_map/reshape | solution.py:234
  78.4 1.8 %slice.383 = bf16[64,8,128]{2,1,0:T(8,128)(2,1)} slice(bf16[64,16,136]{2,1,0:T(8,128)(2,1)} %reshape.133), slice={[0:64], [4:12], [4:132]} | slice | bytes 262144 | tf_op jit(solution)/shard_map/slice | solution.py:234
  83.5 2.5 %fusion.58 = (bf16[64,2176]{1,0:T(8,128)(2,1)}, f32[64,2176]{1,0:T(8,128)S(1)}, bf16[64,2176]{1,0:T(8,128)(2,1)S(1)}, f32[64,2176]{1,0:T(8,128)}) fusion(f32[64,2176]{1,0:T(8,128)S(1)} %copy-done.17, f32[64,2176]{1,0:T(8,128)S(1)} %copy-done.11, bf16[64,2176]{1,0:T(8,128)(2,1)S(1)} %slice.314, bf16[64,1728]{1,0:T(8,128)(2,1)S(1)} %reshape.134, ...), kind=kOutput, calls=%fused_computation.157 | convolution fusion | flops 483246080 | bytes 11919360 | tf_op jit(solution)/shard_map/dot_general | solution.py:54
  86.1 1.5 multiply_convert_fusion.1
  88.2 1.8 %convolution_add_fusion = f32[192,576]{1,0:T(8,128)} fusion(f32[192,576]{1,0:T(8,128)S(1)} %copy-done.29, bf16[576,2176]{1,0:T(8,128)(2,1)S(1)} %copy-done.10, pred[2176]{0:T(1024)(128)(4,1)S(1)} %copy-done.28, bf16[64,2176]{1,0:T(8,128)(2,1)S(1)} %get-tuple-element.18, bf16[64,2176]{1,0:T(8,128)(2,1)S(1)} %get-tuple-element.17, ...), kind=kOutput, calls=%fused_computation.9 | convolution fusion | flops 484331520 | bytes 4229248 | tf_op jit(solution)/shard_map/dot_general | solution.py:60
  90.1 2.1 %copy.11 = f32[192,576]{0,1:T(8,128)} copy(f32[192,576]{1,0:T(8,128)} %convolution_add_fusion) | data formatting | bytes 884736 | tf_op jit(solution)/shard_map/add | solution.py:227
  92.1 3.1 %convolution_add_fusion.1 = f32[192,576]{1,0:T(8,128)} fusion(f32[192,576]{1,0:T(8,128)} %fusion.2, bf16[576,2176]{1,0:T(8,128)(2,1)S(1)} %copy-done.8, bf16[64,2176]{1,0:T(8,128)(2,1)} %get-tuple-element.8, pred[2176]{0:T(1024)(128)(4,1)S(1)} %copy-done.28, bf16[64,2176]{1,0:T(8,128)(2,1)} %copy-done.20, bf16[64,2176]{1,0:T(8,128)(2,1)} %copy-done.19), kind=kOutput, calls=%fused_computation.10 | convolution fusion | flops 484331520 | bytes 4229248 | tf_op jit(solution)/shard_map/dot_general | solution.py:60
  95.2 1.2 copy.10
  96.5 2.2 %pad_maximum_fusion = f32[2,9,192,64]{2,3,1,0:T(8,128)} fusion(f32[1,9,192,64]{2,3,1,0:T(8,128)} %bitcast.61, f32[1,9,192,64]{2,3,1,0:T(8,128)S(1)} %bitcast.62), kind=kLoop, calls=%fused_computation.11 | loop fusion | flops 221184 | bytes 1769472 | tf_op jit(solution)/shard_map/stack | solution.py:141
  98.7 1.8 %copy.12 = f32[2,9,192,64]{3,2,1,0:T(8,128)S(1)} copy(f32[2,9,192,64]{2,3,1,0:T(8,128)} %pad_maximum_fusion) | data formatting | bytes 1769472 | tf_op jit(solution)/shard_map/stack | solution.py:141
  100.8 1.1 pad.30
  101.9 57.7 %shard_map.84 = f32[16,16,8,128]{3,2,1,0:T(8,128)} custom-call(f32[16,128,128]{2,1,0:T(8,128)} %bitcast.56), custom_call_target="tpu_custom_call" | custom-call | tf_op jit(solution)/shard_map/pallas_call | solution.py:150
  159.6 1.2 slice_multiply_fusion
  161.0 1.2 copy.14
  162.4 1.2 copy.13
  166.5 1.4 fusion
  168.0 1.4 reshape.135
  169.4 0.8 slice.385
  (136 shorter events, 16.2 us)
Async XLA Ops:
  0.6 60.4 %copy-start = (bf16[9,192,64]{1,2,0:T(8,128)(2,1)S(1)}, bf16[9,192,64]{1,2,0:T(8,128)(2,1)}, u32[]{:S(2)}) copy-start(bf16[9,192,64]{1,2,0:T(8,128)(2,1)} %param.7) | copy-start | bytes 663556
  1.8 31.9 %copy-start.15 = (bf16[9,192,64]{1,2,0:T(8,128)(2,1)S(1)}, bf16[9,192,64]{1,2,0:T(8,128)(2,1)}, u32[]{:S(2)}) copy-start(bf16[9,192,64]{1,2,0:T(8,128)(2,1)} %param.8) | copy-start | bytes 663556
  2.8 41.7 %collective-permute-start.1 = (bf16[256,4,128]{2,1,0:T(4,128)(2,1)}, bf16[256,4,128]{2,1,0:T(4,128)(2,1)}, u32[]{:S(2)}, u32[]{:S(2)}) collective-permute-start(bf16[256,4,128]{2,1,0:T(4,128)(2,1)} %get-tuple-element.32), channel_id=1, source_target_pairs={{0,16},{1,17},{2,18},{3,19},{4,20},{5,21},{6,22},{7,23},{8,24},{9,... | collective-permute-start | bytes 786440 | tf_op jit(solution)/shard_map/ppermute | solution.py:27
  7.3 37.2 %copy-start.21 = (bf16[2,64,8,128]{3,2,1,0:T(8,128)(2,1)S(1)}, bf16[2,64,8,128]{3,2,1,0:T(8,128)(2,1)}, u32[]{:S(2)}) copy-start(bf16[2,64,8,128]{3,2,1,0:T(8,128)(2,1)} %param.5) | copy-start | bytes 786436
  7.3 37.2 %copy-start.22 = (bf16[64,8,128]{2,1,0:T(8,128)(2,1)S(1)}, bf16[64,8,128]{2,1,0:T(8,128)(2,1)}, u32[]{:S(2)}) copy-start(bf16[64,8,128]{2,1,0:T(8,128)(2,1)} %param.9) | copy-start | bytes 393220
  7.3 37.2 %copy-start.23 = (bf16[64,8,128]{2,1,0:T(8,128)(2,1)S(1)}, bf16[64,8,128]{2,1,0:T(8,128)(2,1)}, u32[]{:S(2)}) copy-start(bf16[64,8,128]{2,1,0:T(8,128)(2,1)} %param.6) | copy-start | bytes 393220
  7.4 37.1 %collective-permute-start.6 = (bf16[256,4,128]{2,1,0:T(4,128)(2,1)}, bf16[256,4,128]{2,1,0:T(4,128)(2,1)}, u32[]{:S(2)}, u32[]{:S(2)}) collective-permute-start(bf16[256,4,128]{2,1,0:T(4,128)(2,1)} %get-tuple-element.33), channel_id=1, source_target_pairs={{16,0},{17,1},{18,2},{19,3},{20,4},{21,5},{22,6},{23,7},{24,8},{25... | collective-permute-start | bytes 786440 | tf_op jit(solution)/shard_map/ppermute | solution.py:27
  11.3 9.5 %collective-permute-start = (bf16[256,4,4]{2,1,0:T(4,128)(2,1)S(1)}, bf16[256,4,4]{2,1,0:T(4,128)(2,1)S(1)}, u32[]{:S(2)}, u32[]{:S(2)}) collective-permute-start(bf16[256,4,4]{2,1,0:T(4,128)(2,1)S(1)} %get-tuple-element.28), channel_id=1, source_target_pairs={{0,17},{1,18},{2,19},{3,20},{4,21},{5,22},{6,23},{7,24},{8,25},{9,... | collective-permute-start | bytes 24584 | tf_op jit(solution)/shard_map/ppermute | solution.py:27
  15.6 8.0 %collective-permute-start.5 = (bf16[256,4,4]{2,1,0:T(4,128)(2,1)S(1)}, bf16[256,4,4]{2,1,0:T(4,128)(2,1)S(1)}, u32[]{:S(2)}, u32[]{:S(2)}) collective-permute-start(bf16[256,4,4]{2,1,0:T(4,128)(2,1)S(1)} %get-tuple-element.29), channel_id=1, source_target_pairs={{16,1},{17,2},{18,3},{19,4},{20,5},{21,6},{22,7},{23,8},{24,9},{25... | collective-permute-start | bytes 24584 | tf_op jit(solution)/shard_map/ppermute | solution.py:27
  18.0 12.9 %collective-permute-start.7 = (bf16[256,4,4]{2,1,0:T(4,128)(2,1)S(1)}, bf16[256,4,4]{2,1,0:T(4,128)(2,1)S(1)}, u32[]{:S(2)}, u32[]{:S(2)}) collective-permute-start(bf16[256,4,4]{2,1,0:T(4,128)(2,1)S(1)} %get-tuple-element.30), channel_id=1, source_target_pairs={{17,0},{18,1},{19,2},{20,3},{21,4},{22,5},{23,6},{24,7},{25,8},{26... | collective-permute-start | bytes 24584 | tf_op jit(solution)/shard_map/ppermute | solution.py:27
  20.8 12.9 %copy-start.24 = (bf16[256,4,4]{2,1,0:T(4,128)(2,1)}, bf16[256,4,4]{2,1,0:T(4,128)(2,1)S(1)}, u32[]{:S(2)}) copy-start(bf16[256,4,4]{2,1,0:T(4,128)(2,1)S(1)} %collective-permute-done) | copy-start | bytes 24580
  20.8 13.5 %collective-permute-start.2 = (bf16[256,4,4]{2,1,0:T(4,128)(2,1)}, bf16[256,4,4]{2,1,0:T(4,128)(2,1)}, u32[]{:S(2)}, u32[]{:S(2)}) collective-permute-start(bf16[256,4,4]{2,1,0:T(4,128)(2,1)} %get-tuple-element.31), channel_id=1, source_target_pairs={{1,16},{2,17},{3,18},{4,19},{5,20},{6,21},{7,22},{8,23},{9,24},{10... | collective-permute-start | bytes 24584 | tf_op jit(solution)/shard_map/ppermute | solution.py:27
  23.6 10.1 %copy-start.25 = (bf16[256,4,4]{2,1,0:T(4,128)(2,1)}, bf16[256,4,4]{2,1,0:T(4,128)(2,1)S(1)}, u32[]{:S(2)}) copy-start(bf16[256,4,4]{2,1,0:T(4,128)(2,1)S(1)} %collective-permute-done.5) | copy-start | bytes 24580
  23.6 17.0 %collective-permute-start.3 = (bf16[256,8,4]{2,1,0:T(8,128)(2,1)}, bf16[256,8,4]{2,1,0:T(8,128)(2,1)S(1)}, u32[]{:S(2)}, u32[]{:S(2)}) collective-permute-start(bf16[256,8,4]{2,1,0:T(8,128)(2,1)} %get-tuple-element.34), channel_id=1, source_target_pairs={{0,1},{1,2},{2,3},{3,4},{4,5},{5,6},{6,7},{7,8},{8,9},{9,10},{10,1... | collective-permute-start | bytes 49160 | tf_op jit(solution)/shard_map/ppermute | solution.py:27
  30.9 2.8 %copy-start.26 = (bf16[256,4,4]{2,1,0:T(4,128)(2,1)}, bf16[256,4,4]{2,1,0:T(4,128)(2,1)S(1)}, u32[]{:S(2)}) copy-start(bf16[256,4,4]{2,1,0:T(4,128)(2,1)S(1)} %collective-permute-done.7) | copy-start | bytes 24580
  30.9 13.5 %collective-permute-start.4 = (bf16[256,8,4]{2,1,0:T(8,128)(2,1)S(1)}, bf16[256,8,4]{2,1,0:T(8,128)(2,1)S(1)}, u32[]{:S(2)}, u32[]{:S(2)}) collective-permute-start(bf16[256,8,4]{2,1,0:T(8,128)(2,1)S(1)} %get-tuple-element.35), channel_id=1, source_target_pairs={{1,0},{2,1},{3,2},{4,3},{5,4},{6,5},{7,6},{8,7},{9,8},{10,9},{11,1... | collective-permute-start | bytes 49160 | tf_op jit(solution)/shard_map/ppermute | solution.py:27
  34.3 48.6 %copy-start.13 = (bf16[64,1728]{1,0:T(8,128)(2,1)}, bf16[64,1728]{1,0:T(8,128)(2,1)S(1)}, u32[]{:S(2)}) copy-start(bf16[64,1728]{1,0:T(8,128)(2,1)S(1)} %reshape.134) | copy-start | bytes 663556
  59.8 1.4 copy-start.7
  61.0 1.5 copy-start.9
  61.2 1.3 copy-start.16
  62.1 1.3 copy-start.2
  62.5 0.9 copy-start.27
  68.1 1.1 copy-start.3
  69.6 1.3 copy-start.5
  70.6 0.7 copy-start.28
  81.9 1.1 copy-start.4
  82.0 1.2 copy-start.6
  82.0 1.4 copy-start.11
  82.0 1.5 copy-start.17
  86.0 1.6 copy-start.19
  86.0 2.2 %copy-start.10 = (bf16[576,2176]{1,0:T(8,128)(2,1)S(1)}, bf16[576,2176]{1,0:T(8,128)(2,1)}, u32[]{:S(2)}) copy-start(bf16[576,2176]{1,0:T(8,128)(2,1)} %copy-done.9) | copy-start | bytes 7520260
  86.1 2.2 %copy-start.29 = (f32[192,576]{1,0:T(8,128)S(1)}, f32[192,576]{1,0:T(8,128)}, u32[]{:S(2)}) copy-start(f32[192,576]{1,0:T(8,128)} %fusion.6) | copy-start | bytes 1327108
  87.5 0.7 copy-start.20
  88.2 3.9 %copy-start.8 = (bf16[576,2176]{1,0:T(8,128)(2,1)S(1)}, bf16[576,2176]{1,0:T(8,128)(2,1)}, u32[]{:S(2)}) copy-start(bf16[576,2176]{1,0:T(8,128)(2,1)} %copy-done.7) | copy-start | bytes 7520260
  165.2 1.1 copy-start.12
  165.3 1.1 copy-start.14
  165.3 1.3 copy-start.18
  166.5 3.7 %copy-start.1 = (bf16[9,192,64]{1,2,0:T(8,128)(2,1)S(1)}, bf16[9,192,64]{1,2,0:T(8,128)(2,1)}, u32[]{:S(2)}) copy-start(bf16[9,192,64]{1,2,0:T(8,128)(2,1)} %param.7) | copy-start | bytes 663556

commit v2 on v0

--- a/solution.py
+++ b/solution.py
@@ -23,31 +23,36 @@
     return array
 
 
-def shifted(flat, offsets, margin, length):
-    return jnp.concatenate([flat[:, margin + off : margin + off + length] for off in offsets], 0)
-
-
-def conv_flat(weights, flat, offsets, margin, length):
+def shifted(field, field_start, out_start, length, offsets):
+    base = out_start - field_start
+    return jnp.concatenate([field[:, base + off : base + off + length] for off in offsets], 0)
+
+
+def conv_flat(weights, field, field_start, span, offsets):
     taps, out_ch, in_ch = weights.shape
-    stack = shifted(flat, offsets, margin, length)
+    stack = shifted(field, field_start, span[0], span[1] - span[0], offsets)
     matrix = weights.transpose(1, 0, 2).reshape(out_ch, taps * in_ch)
     return jnp.dot(matrix, stack, preferred_element_type=jnp.float32)
 
 
-def spread_flat(weights, flat, offsets, margin, length):
+def spread_flat(weights, field, field_start, span, offsets):
     taps, out_ch, in_ch = weights.shape
-    stack = shifted(flat, [-off for off in offsets], margin, length)
+    stack = shifted(field, field_start, span[0], span[1] - span[0], [-off for off in offsets])
     matrix = weights.transpose(2, 0, 1).reshape(in_ch, taps * out_ch)
     return jnp.dot(matrix, stack, preferred_element_type=jnp.float32)
 
 
-def weight_flat(pre_grad, flat, offsets, margin, length):
+def weight_flat(pre_grad, field, field_start, span, offsets):
     taps = len(offsets)
-    stack = shifted(flat, offsets, margin, length)
+    stack = shifted(field, field_start, span[0], span[1] - span[0], offsets)
     share = lax.dot_general(
         pre_grad, stack, (((1,), (1,)), ((), ())), preferred_element_type=jnp.float32
     )
     return share.reshape(pre_grad.shape[0], taps, -1).transpose(1, 0, 2)
+
+
+def cut(field, field_start, span):
+    return field[:, span[0] - field_start : span[1] - field_start]
 
 
 def gates(from_input, from_state, previous, channels):
@@ -161,14 +166,19 @@
     halo = HALO
     ext_rows, ext_cols = rows + 2 * halo, cols + 2 * halo
     length = ext_rows * ext_cols
-    margin = ext_cols + 1
+    reach = ext_cols + 1
     offsets = [(k // 3 - 1) * ext_cols + (k % 3 - 1) for k in range(9)]
+    tile = (halo * ext_cols, (halo + rows) * ext_cols)
+    spans = [(tile[0] - depth * reach, tile[1] + depth * reach) for depth in range(2 * step_count)]
+    forward_spans = spans[2 * step_count - 1 :: -1][:step_count]
+    backward_spans = spans[step_count : 0 : -1]
 
     fields = jnp.concatenate([frames.reshape(-1, rows, cols), state, cotangent], 0)
     fields = padded_2(fields, (("row", 1), ("col", 2)), halo).reshape(-1, length)
-    frame_flat = [fields[t * frames.shape[1] : (t + 1) * frames.shape[1]] for t in range(step_count)]
+    padded = jnp.pad(fields, ((0, 0), (reach, reach)))
+    frame_pad = [padded[t * frames.shape[1] : (t + 1) * frames.shape[1]] for t in range(step_count)]
     base = step_count * frames.shape[1]
-    state_flat = fields[base : base + channels]
+    state_pad = padded[base : base + channels]
     cot_flat = fields[base + channels :]
 
     r = lax.broadcasted_iota(jnp.int32, (ext_rows, ext_cols), 0)
@@ -183,44 +193,53 @@
     ).reshape(1, length)
     own = ((r >= halo) & (r < halo + rows) & (c >= halo) & (c < halo + cols)).reshape(1, length)
 
-    def pad(flat):
-        return jnp.pad(flat, ((0, 0), (margin, margin)))
-
     records = []
-    current = state_flat
+    current, current_start = state_pad, -reach
     for step_index in range(step_count):
-        frame_pad, state_pad = pad(frame_flat[step_index]), pad(current)
-        from_input = conv_flat(input_weight, frame_pad, offsets, margin, length)
-        from_state = conv_flat(state_weight, state_pad, offsets, margin, length)
-        new_state, saved = gates(from_input, from_state, current, channels)
-        records.append((frame_pad, state_pad, current, saved))
-        current = jnp.where(inside, new_state, jnp.zeros_like(new_state))
-
-    grad_state = cot_flat.astype(jnp.float32)
-    input_pres, input_fields, state_pres, state_fields = [], [], [], []
+        span = forward_spans[step_index]
+        from_input = conv_flat(input_weight, frame_pad[step_index], -reach, span, offsets)
+        from_state = conv_flat(state_weight, current, current_start, span, offsets)
+        previous = cut(current, current_start, span)
+        new_state, saved = gates(from_input, from_state, previous, channels)
+        records.append((current, current_start, span, saved))
+        current = jnp.where(cut(inside, 0, span), new_state, jnp.zeros_like(new_state))
+        current_start = span[0]
+    final_state = cut(current, current_start, tile)
+
+    grad_state, grad_start = cot_flat, 0
+    input_sum = None
+    state_sum = None
     for step_index in reversed(range(step_count)):
-        frame_pad, state_pad, previous, saved = records[step_index]
-        input_pre, state_pre, direct = gate_grads(grad_state, saved, previous)
-        input_pres.append(jnp.where(own, input_pre, jnp.zeros_like(input_pre)))
-        state_pres.append(jnp.where(own, state_pre, jnp.zeros_like(state_pre)))
-        input_fields.append(frame_pad)
-        state_fields.append(state_pad)
-        state_pre = jnp.where(inside, state_pre, jnp.zeros_like(state_pre))
-        grad_state = direct + spread_flat(state_weight, pad(state_pre), offsets, margin, length)
-
-    input_sum = sum(
-        weight_flat(p, f, offsets, margin, length) for p, f in zip(input_pres, input_fields)
-    )
-    state_sum = sum(
-        weight_flat(p, f, offsets, margin, length) for p, f in zip(state_pres, state_fields)
-    )
+        field, field_start, forward_span, saved = records[step_index]
+        span = backward_spans[step_count - 1 - step_index]
+        saved = tuple(cut(value, forward_span[0], span) for value in saved)
+        previous = cut(field, field_start, span)
+        input_pre, state_pre, direct = gate_grads(
+            cut(grad_state, grad_start, span).astype(jnp.float32), saved, previous
+        )
+        keep = cut(own, 0, tile)
+        input_tile = cut(input_pre, span[0], tile)
+        state_tile = cut(state_pre, span[0], tile)
+        input_share = weight_flat(
+            jnp.where(keep, input_tile, jnp.zeros_like(input_tile)), frame_pad[step_index], -reach, tile, offsets
+        )
+        state_share = weight_flat(
+            jnp.where(keep, state_tile, jnp.zeros_like(state_tile)), field, field_start, tile, offsets
+        )
+        input_sum = input_share if input_sum is None else input_sum + input_share
+        state_sum = state_share if state_sum is None else state_sum + state_share
+        state_pre = jnp.where(cut(inside, 0, span), state_pre, jnp.zeros_like(state_pre))
+        inner = (span[0] + reach, span[1] - reach)
+        grad_state = cut(direct, span[0], inner) + spread_flat(state_weight, state_pre, span[0], inner, offsets)
+        grad_start = inner[0]
+
     input_sum, state_sum = all_sum([input_sum, state_sum])
     loss_scale = (rows * lax.axis_size("row") * cols * lax.axis_size("col")) ** (-0.5)
 
     def crop(flat):
-        return flat.reshape(-1, ext_rows, ext_cols)[:, halo : halo + rows, halo : halo + cols]
-
-    return (crop(current), crop(grad_state), input_sum * loss_scale, state_sum * loss_scale)
+        return flat.reshape(flat.shape[0], rows, ext_cols)[:, :, halo : halo + cols]
+
+    return (crop(final_state), crop(grad_state), input_sum * loss_scale, state_sum * loss_scale)
 
 
 def solution(mesh):

time: 151 us -> 175 us (1.16)
  local copies, waits for them, and re-layouts: 40.4 us -> 62.4 us
  waiting for transfers between devices: 5.72 us -> 2.52 us
  other arithmetic: 18.5 us -> 21.1 us
    concatenate x6 -> x10, local copies, waits for them, and re-layouts: 1.16 us -> 18.7 us  [the longest x9 15.2 us: shifted(): jnp.concatenate([field[:, base + off:base + off + length] for off in offs...]
    unnamed x108 -> x125, local copies, waits for them, and re-layouts: 14.2 us -> 22.2 us
    slice x5 -> x13, local copies, waits for them, and re-layouts: 5.73 us -> 11.1 us  [the longest x3 7.83 us: shifted(): field[:, base + off:base + off + length]]
    another operation x4 -> x5, other arithmetic: 2.24 us -> 6.74 us
    ppermute x2, waiting for transfers between devices: 4.52 us -> 0.7 us  [padded_2(): after = lax.ppermute(first, axis, down)]
    ppermute x2, starting transfers between devices: 3.23 us -> 6.43 us  [padded_2(): after = lax.ppermute(first, axis, down)]
    dot_general x4, matrix products: 3.52 us -> 6.4 us  [conv_flat(): return jnp.dot(matrix, stack, preferred_element_type=jnp.float32)]
    add x2, local copies, waits for them, and re-layouts: 3.3 us -> 0.43 us  [the longest x1 0.21 us: local(): state_sum = state_share if state_sum is None else state_sum + state_share]
  transfers between devices with their start and end apart: 4 -> 4, of which waited for: 2 -> 2; matrix products, arithmetic and copies ran while one was open for 2% -> 3% of each run, Pallas kernels for 0% -> 0%
where the time goes in v2:
time: 175 us; the launch traced here: 174 us
  local copies, waits for them, and re-layouts  62.4 us (36%)
  Pallas kernels  56.9 us (33%)
  other arithmetic  21.1 us (12%)
  matrix products  17 us (10%)
  starting transfers between devices  12.3 us (7%)
  waiting for transfers between devices  2.52 us (1%)
    pallas_call x1, Pallas kernels, all_sum(): pl.pallas_call(functools.partial(reduce_kernel, rows, cols), out_shape=ja...  56.9 us
    unnamed x125, local copies, waits for them, and re-layouts  22.2 us
    concatenate x9, local copies, waits for them, and re-layouts, shifted(): jnp.concatenate([field[:, base + off:base + off + length] for off in offs...  15.2 us
    dot_general x4, matrix products, weight_flat(): lax.dot_general(pre_grad, stack, (((1,), (1,)), ((), ())), preferred_elem...  8.87 us
    slice x3, local copies, waits for them, and re-layouts, shifted(): field[:, base + off:base + off + length]  7.83 us
    another operation x5, other arithmetic  6.74 us
    concatenate x2, other arithmetic, padded_2(): array = jnp.concatenate([before, array, after], axis=dim)  6.65 us
    ppermute x2, starting transfers between devices, padded_2(): after = lax.ppermute(first, axis, down)  6.43 us
  transfers between devices with their start and end apart: 4, of which 2 were waited for; matrix products, arithmetic and copies ran while one was open for 3% of the time, Pallas kernels for 0%

profile of v2, /device:TPU:1, one launch (start us, length us, event | category | flops | bytes accessed | tf_op | source)
XLA Modules:
  0.0 173.8 jit_solution(14560015999534237285)
XLA Ops:
  0.7 1.2 pad_maximum_fusion.5
  2.1 5.1 %collective-permute-start.1 = (bf16[256,4,128]{2,1,0:T(4,128)(2,1)S(1)}, bf16[256,4,128]{2,1,0:T(4,128)(2,1)S(1)}, u32[]{:S(2)}, u32[]{:S(2)}) collective-permute-start(bf16[256,4,128]{2,1,0:T(4,128)(2,1)S(1)} %get-tuple-element.78), channel_id=1, source_target_pairs={{16,0},{32,16},{48,32},{64,48},{80,64},{96,80},{112,96},{128,112},... | collective-permute-start | bytes 786440 | tf_op jit(solution)/shard_map/ppermute | solution.py:21
  7.2 1.9 %collective-permute-start = (bf16[256,4,128]{2,1,0:T(4,128)(2,1)S(1)}, bf16[256,4,128]{2,1,0:T(4,128)(2,1)S(1)}, u32[]{:S(2)}, u32[]{:S(2)}) collective-permute-start(bf16[256,4,128]{2,1,0:T(4,128)(2,1)S(1)} %get-tuple-element.77), channel_id=1, source_target_pairs={{0,16},{16,32},{32,48},{48,64},{64,80},{80,96},{96,112},{112,128},... | collective-permute-start | bytes 786440 | tf_op jit(solution)/shard_map/ppermute | solution.py:20
  10.6 1.8 %collective-permute-done = bf16[256,4,128]{2,1,0:T(4,128)(2,1)S(1)} collective-permute-done((bf16[256,4,128]{2,1,0:T(4,128)(2,1)S(1)}, bf16[256,4,128]{2,1,0:T(4,128)(2,1)S(1)}, u32[]{:S(2)}, u32[]{:S(2)}) %collective-permute-start) | collective-permute-done | bytes 262176 | tf_op jit(solution)/shard_map/ppermute | solution.py:20
  14.3 0.9 copy.43
  15.2 1.3 collective-permute-start.3
  16.5 0.9 copy.42
  17.4 4.0 %collective-permute-start.2 = (bf16[256,16,4]{0,1,2:T(8,128)(2,1)S(1)}, bf16[256,16,4]{0,1,2:T(8,128)(2,1)S(1)}, u32[]{:S(2)}, u32[]{:S(2)}) collective-permute-start(bf16[256,16,4]{0,1,2:T(8,128)(2,1)S(1)} %copy.42), channel_id=1, source_target_pairs={{0,1},{1,2},{2,3},{3,4},{4,5},{5,6},{6,7},{7,8},{8,9},{9,10},{10,1... | collective-permute-start | bytes 98312 | tf_op jit(solution)/shard_map/ppermute | solution.py:20
  22.3 1.0 reshape.171
  23.4 1.0 copy.45
  24.4 1.0 copy.44
  25.4 6.1 %pad_maximum_fusion = bf16[256,16,136]{2,1,0:T(8,128)(2,1)} fusion(bf16[256,16,4]{2,1,0:T(8,128)(2,1)S(1)} %copy.45, bf16[256,4,128]{2,1,0:T(4,128)(2,1)} %copy-done.30, bf16[64,8,128]{2,1,0:T(8,128)(2,1)} %param.9, bf16[64,8,128]{2,1,0:T(8,128)(2,1)} %param.6, bf16[128,8,128]{2,1,0:T(8,128)(2,1)S(1)} %bitcast.70, bf16[256,4,128]{2,1,0:T(4,128)(2,1)} %copy-done.31, ...), kind=kLoop, calls=%fused_computation.8 | loop fusion | flops 7798784 | bytes 2228224 | tf_op jit(solution)/shard_map/concatenate | solution.py:22
  31.5 3.5 %copy.46 = bf16[256,16,136]{0,2,1:T(8,128)(2,1)S(1)} copy(bf16[256,16,136]{2,1,0:T(8,128)(2,1)} %pad_maximum_fusion) | data formatting | bytes 2228224 | tf_op jit(solution)/shard_map/concatenate | solution.py:22
  35.0 1.0 copy.47
  36.0 3.3 %fusion.79 = (bf16[64,1636]{0,1:T(8,128)(2,1)}, bf16[64,1636]{0,1:T(8,128)(2,1)}, bf16[64,1636]{0,1:T(8,128)(2,1)}, bf16[64,1636]{0,1:T(8,128)(2,1)}, bf16[64,16...) fusion(bf16[256,2176]{0,1:T(8,128)(2,1)S(1)} %bitcast.58), kind=kLoop, calls=%fused_computation.183 | loop fusion | bytes 3769344 | tf_op jit(solution)/shard_map/slice | solution.py:28
  43.8 1.5 fusion.44
  46.7 3.0 %fusion.77 = (bf16[64,1088]{0,1:T(8,128)(2,1)}, bf16[64,1088]{0,1:T(8,128)(2,1)}, bf16[64,1088]{0,1:T(8,128)(2,1)}, bf16[64,1088]{0,1:T(8,128)(2,1)}, bf16[64,10...) fusion(bf16[256,2176]{0,1:T(8,128)(2,1)S(1)} %bitcast.59), kind=kLoop, calls=%fused_computation.181 | loop fusion | bytes 5292032 | tf_op jit(solution)/shard_map/slice | solution.py:28
  49.8 1.5 fusion.78
  52.9 0.8 slice_dynamic-update-slice_fusion.28
  53.7 0.8 slice_dynamic-update-slice_fusion.32
  54.6 0.8 slice_dynamic-update-slice_fusion.27
  56.2 0.8 slice_dynamic-update-slice_fusion.25
  57.0 1.0 slice_dynamic-update-slice_fusion.24
  58.7 2.4 %convolution_bitcast_fusion.1 = f32[192,1636]{1,0:T(8,128)S(1)} fusion(bf16[576,1636]{1,0:T(8,128)(2,1)} %get-tuple-element.82, bf16[192,576]{0,1:T(8,128)(2,1)S(1)} %bitcast.65), kind=kOutput, calls=%fused_computation.1 | convolution fusion | flops 361857024 | bytes 3362304 | tf_op jit(solution)/shard_map/dot_general | solution.py:35
  61.1 5.7 %concatenate.58 = bf16[576,1636]{0,1:T(8,128)(2,1)} concatenate(bf16[64,1636]{0,1:T(8,128)(2,1)} %get-tuple-element.64, bf16[64,1636]{0,1:T(8,128)(2,1)} %get-tuple-element.63, bf16[64,1636]{0,1:T(8,128)(2,1)} %get-tuple-element.62, bf16[64,1636]{0,1:T(8,128)(2,1)} %get-tuple-element.61, bf16[64,1636]{0,1:T(8,128)(2,1)} %get-tuple-element.60, ...), dimensions={0} | concatenate | bytes 3769344 | tf_op jit(solution)/shard_map/concatenate | solution.py:28
  66.7 2.4 %convolution_bitcast_fusion = f32[192,1636]{1,0:T(8,128)S(1)} fusion(bf16[576,1636]{0,1:T(8,128)(2,1)} %concatenate.58, bf16[192,576]{0,1:T(8,128)(2,1)S(1)} %bitcast.55), kind=kOutput, calls=%fused_computation | convolution fusion | flops 361857024 | bytes 3362304 | tf_op jit(solution)/shard_map/dot_general | solution.py:35
  69.2 1.0 slice_convert_fusion
  70.2 2.2 %fusion.71 = (bf16[64,1636]{1,0:T(8,128)(2,1)}, f32[64,1636]{1,0:T(8,128)}, f32[64,1636]{1,0:T(8,128)S(1)}, f32[64,1636]{1,0:T(8,128)S(1)}) fusion(bf16[64,2176]{1,0:T(8,128)(2,1)} %copy-done.4, f32[192,1636]{1,0:T(8,128)S(1)} %convolution_bitcast_fusion.1, f32[192,1636]{1,0:T(8,128)S(1)} %convolution_bitcast_fusion), kind=kLoop, calls=%fused_computation.180 | loop fusion | flops 1779968 | bytes 4188160 | tf_op jit(solution)/shard_map/convert.5
  72.5 0.9 multiply_convert_fusion.2
  74.9 1.3 multiply_convert_fusion.1
  76.2 1.0 fusion.2
  79.5 0.9 fusion
  80.7 1.0 fusion.70
  81.7 1.3 fusion.41
  84.8 0.8 fusion.1
  86.0 0.8 slice.708
  93.0 2.7 %fusion.23 = f32[192,576]{1,0:T(8,128)} fusion(bf16[576,1088]{1,0:T(8,128)(2,1)} %slice_dynamic-update-slice_fusion.33, bf16[192,1636]{1,0:T(8,128)(2,1)S(1)} %copy-done.36, pred[1088]{0:T(1024)(128)(4,1)S(1)} %copy-done.37), kind=kOutput, calls=%fused_computation.70 | convolution fusion | flops 240857088 | bytes 2140160 | tf_op jit(solution)/shard_map/dot_general | solution.py:48
  95.8 2.7 %concatenate.71 = bf16[576,1088]{0,1:T(8,128)(2,1)S(1)} concatenate(bf16[64,1088]{0,1:T(8,128)(2,1)S(1)} %copy-done.26, bf16[64,1088]{0,1:T(8,128)(2,1)S(1)} %copy-done.25, bf16[64,1088]{0,1:T(8,128)(2,1)S(1)} %copy-done.27, bf16[64,1088]{0,1:T(8,128)(2,1)S(1)} %copy-done.28, bf16[64,1088]{0,1:T(8,128)(2,1)S(1)} %copy-done.29, bf16[64,1088]{0,1:T(8,128)(2,1)} %get-tuple-element.52, ...), dimensions={0} | concatenate | bytes 2506752 | tf_op jit(solution)/shard_map/concatenate | solution.py:28
  98.5 1.7 convolution_add_fusion
  100.5 2.7 %concatenate.67 = bf16[576,1088]{0,1:T(8,128)(2,1)S(1)} concatenate(bf16[64,1088]{0,1:T(8,128)(2,1)} %get-tuple-element.48, bf16[64,1088]{0,1:T(8,128)(2,1)} %get-tuple-element.47, bf16[64,1088]{0,1:T(8,128)(2,1)} %get-tuple-element.46, bf16[64,1088]{0,1:T(8,128)(2,1)} %get-tuple-element.45, bf16[64,1088]{0,1:T(8,128)(2,1)} %get-tuple-element.44, ...), dimensions={0} | concatenate | bytes 2506752 | tf_op jit(solution)/shard_map/concatenate | solution.py:28
  103.2 2.6 %fusion.21 = f32[192,576]{1,0:T(8,128)} fusion(bf16[576,1088]{0,1:T(8,128)(2,1)S(1)} %concatenate.67, bf16[64,1636]{1,0:T(8,128)(2,1)} %get-tuple-element.80, bf16[64,1636]{1,0:T(8,128)(2,1)} %copy-done.32, bf16[64,1636]{1,0:T(8,128)(2,1)} %get-tuple-element.18, pred[1088]{0:T(1024)(128)(4,1)S(1)} %copy-done.37), kind=kOutput, calls=%fused_computation.65 | convolution fusion | flops 242110464 | bytes 2325056 | tf_op jit(solution)/shard_map/dot_general | solution.py:48
  105.8 2.9 %concatenate.69 = bf16[576,1088]{0,1:T(8,128)(2,1)S(1)} concatenate(bf16[64,1088]{0,1:T(8,128)(2,1)} %get-tuple-element.39, bf16[64,1088]{0,1:T(8,128)(2,1)} %get-tuple-element.38, bf16[64,1088]{0,1:T(8,128)(2,1)} %get-tuple-element.37, bf16[64,1088]{0,1:T(8,128)(2,1)} %get-tuple-element.36, bf16[64,1088]{0,1:T(8,128)(2,1)S(1)} %copy-done.20, bf16[64,1088]{0,1:T(8,128)(2,1)S(1)} %copy-done.19, ...), dimensions={0} | concatenate | bytes 2506752 | tf_op jit(solution)/shard_map/concatenate | solution.py:28
  108.8 1.9 %convolution_add_fusion.1 = f32[192,576]{1,0:T(8,128)S(1)} fusion(f32[192,576]{1,0:T(8,128)} %fusion.21, bf16[576,1088]{0,1:T(8,128)(2,1)S(1)} %concatenate.69, bf16[64,1362]{1,0:T(8,128)(2,1)} %copy-done.34, bf16[64,1362]{1,0:T(8,128)(2,1)} %copy-done.35, bf16[64,1362]{1,0:T(8,128)(2,1)} %get-tuple-element.16, pred[1088]{0:T(1024)(128)(4,1)S(1)} %copy-done.37), kind=kOutput, calls=%fused_computation.10 | convolution fusion | flops 242221056 | bytes 2662208 | tf_op jit(solution)/shard_map/dot_general | solution.py:48
  111.8 1.1 pad.9
  112.9 56.9 %shard_map.84 = f32[16,16,8,128]{3,2,1,0:T(8,128)} custom-call(f32[16,128,128]{2,1,0:T(8,128)} %bitcast.61), custom_call_target="tpu_custom_call" | custom-call | tf_op jit(solution)/shard_map/pallas_call | solution.py:142
  169.8 1.2 slice_multiply_fusion.1
  171.2 1.2 copy.59
  172.6 1.2 copy.60
  (161 shorter events, 27.4 us)
Async XLA Ops:
  0.6 42.0 %copy-start = (bf16[9,192,64]{1,2,0:T(8,128)(2,1)S(1)}, bf16[9,192,64]{1,2,0:T(8,128)(2,1)}, u32[]{:S(2)}) copy-start(bf16[9,192,64]{1,2,0:T(8,128)(2,1)} %param.7) | copy-start | bytes 663556
  0.6 12.5 %copy-start.14 = (bf16[64,8,128]{2,1,0:T(8,128)(2,1)S(1)}, bf16[64,8,128]{2,1,0:T(8,128)(2,1)}, u32[]{:S(2)}) copy-start(bf16[64,8,128]{2,1,0:T(8,128)(2,1)} %param.9) | copy-start | bytes 393220
  0.7 12.5 %copy-start.15 = (bf16[64,8,128]{2,1,0:T(8,128)(2,1)S(1)}, bf16[64,8,128]{2,1,0:T(8,128)(2,1)}, u32[]{:S(2)}) copy-start(bf16[64,8,128]{2,1,0:T(8,128)(2,1)} %param.6) | copy-start | bytes 393220
  0.7 12.5 %copy-start.7 = (bf16[2,64,8,128]{3,2,1,0:T(8,128)(2,1)S(1)}, bf16[2,64,8,128]{3,2,1,0:T(8,128)(2,1)}, u32[]{:S(2)}) copy-start(bf16[2,64,8,128]{3,2,1,0:T(8,128)(2,1)} %param.5) | copy-start | bytes 786436
  2.1 8.6 %collective-permute-start.1 = (bf16[256,4,128]{2,1,0:T(4,128)(2,1)S(1)}, bf16[256,4,128]{2,1,0:T(4,128)(2,1)S(1)}, u32[]{:S(2)}, u32[]{:S(2)}) collective-permute-start(bf16[256,4,128]{2,1,0:T(4,128)(2,1)S(1)} %get-tuple-element.78), channel_id=1, source_target_pairs={{16,0},{32,16},{48,32},{64,48},{80,64},{96,80},{112,96},{128,112},... | collective-permute-start | bytes 786440 | tf_op jit(solution)/shard_map/ppermute | solution.py:21
  7.2 5.2 %collective-permute-start = (bf16[256,4,128]{2,1,0:T(4,128)(2,1)S(1)}, bf16[256,4,128]{2,1,0:T(4,128)(2,1)S(1)}, u32[]{:S(2)}, u32[]{:S(2)}) collective-permute-start(bf16[256,4,128]{2,1,0:T(4,128)(2,1)S(1)} %get-tuple-element.77), channel_id=1, source_target_pairs={{0,16},{16,32},{32,48},{48,64},{64,80},{80,96},{96,112},{112,128},... | collective-permute-start | bytes 786440 | tf_op jit(solution)/shard_map/ppermute | solution.py:20
  10.6 1.8 %copy-start.30 = (bf16[256,4,128]{2,1,0:T(4,128)(2,1)}, bf16[256,4,128]{2,1,0:T(4,128)(2,1)S(1)}, u32[]{:S(2)}) copy-start(bf16[256,4,128]{2,1,0:T(4,128)(2,1)S(1)} %collective-permute-done.1) | copy-start | bytes 786436
  12.5 0.7 copy-start.31
  14.2 7.9 %copy-start.6 = (bf16[9,192,64]{1,2,0:T(8,128)(2,1)S(1)}, bf16[9,192,64]{1,2,0:T(8,128)(2,1)}, u32[]{:S(2)}) copy-start(bf16[9,192,64]{1,2,0:T(8,128)(2,1)} %param.8) | copy-start | bytes 663556
  15.2 8.2 %collective-permute-start.3 = (bf16[256,16,4]{0,1,2:T(8,128)(2,1)S(1)}, bf16[256,16,4]{0,1,2:T(8,128)(2,1)S(1)}, u32[]{:S(2)}, u32[]{:S(2)}) collective-permute-start(bf16[256,16,4]{0,1,2:T(8,128)(2,1)S(1)} %copy.43), channel_id=1, source_target_pairs={{1,0},{2,1},{3,2},{4,3},{5,4},{6,5},{7,6},{8,7},{9,8},{10,9},{11,1... | collective-permute-start | bytes 98312 | tf_op jit(solution)/shard_map/ppermute | solution.py:21
  17.4 7.0 %collective-permute-start.2 = (bf16[256,16,4]{0,1,2:T(8,128)(2,1)S(1)}, bf16[256,16,4]{0,1,2:T(8,128)(2,1)S(1)}, u32[]{:S(2)}, u32[]{:S(2)}) collective-permute-start(bf16[256,16,4]{0,1,2:T(8,128)(2,1)S(1)} %copy.42), channel_id=1, source_target_pairs={{0,1},{1,2},{2,3},{3,4},{4,5},{5,6},{6,7},{7,8},{8,9},{9,10},{10,1... | collective-permute-start | bytes 98312 | tf_op jit(solution)/shard_map/ppermute | solution.py:20
  42.6 1.2 copy-start.2
  51.3 6.7 %slice-start = ((bf16[256,16,136]{2,1,0:T(8,128)(2,1)}), bf16[64,16,136]{2,1,0:T(8,128)(2,1)S(1)}, s32[]{:S(2)}) async-start(bf16[256,16,136]{2,1,0:T(8,128)(2,1)} %pad_maximum_fusion), calls=%async_computation | async-start | bytes 1048576 | tf_op jit(solution)/shard_map/slice | solution.py:182
  58.7 10.5 %copy-start.4 = (bf16[64,2176]{1,0:T(8,128)(2,1)}, bf16[64,2176]{1,0:T(8,128)(2,1)S(1)}, u32[]{:S(2)}) copy-start(bf16[64,2176]{1,0:T(8,128)(2,1)S(1)} %slice.560) | copy-start | bytes 835588
  69.2 3.3 %copy-start.3 = (f32[192,1636]{1,0:T(8,128)}, f32[192,1636]{1,0:T(8,128)S(1)}, u32[]{:S(2)}) copy-start(f32[192,1636]{1,0:T(8,128)S(1)} %convolution_bitcast_fusion) | copy-start | bytes 3769348
  70.2 2.2 %copy-start.5 = (bf16[64,2176]{1,0:T(8,128)(2,1)S(1)}, bf16[64,2176]{1,0:T(8,128)(2,1)}, u32[]{:S(2)}) copy-start(bf16[64,2176]{1,0:T(8,128)(2,1)} %copy-done.4) | copy-start | bytes 835588
  70.2 3.2 %copy-start.13 = (f32[64,1636]{1,0:T(8,128)S(1)}, f32[64,1636]{1,0:T(8,128)}, u32[]{:S(2)}) copy-start(f32[64,1636]{1,0:T(8,128)} %get-tuple-element.83) | copy-start | bytes 1256452
  74.1 2.1 %copy-start.33 = (bf16[64,1636]{1,0:T(8,128)(2,1)S(1)}, bf16[64,1636]{1,0:T(8,128)(2,1)}, u32[]{:S(2)}) copy-start(bf16[64,1636]{1,0:T(8,128)(2,1)} %get-tuple-element.80) | copy-start | bytes 628228
  76.2 1.7 copy-start.32
  78.4 0.9 copy-start.8
  78.4 1.1 copy-start.9
  79.5 1.0 copy-start.10
  79.5 1.2 copy-start.11
  80.4 1.3 copy-start.12
  81.7 1.5 copy-start.34
  83.0 0.7 copy-start.35
  85.6 7.4 %copy-start.37 = (pred[1088]{0:T(1024)(128)(4,1)S(1)}, pred[1088]{0:T(1024)(128)(4,1)}, u32[]{:S(2)}) copy-start(pred[1088]{0:T(1024)(128)(4,1)} %slice_reduce_fusion.3) | copy-start | bytes 3268
  86.0 7.0 %copy-start.36 = (bf16[192,1636]{1,0:T(8,128)(2,1)S(1)}, bf16[192,1636]{1,0:T(8,128)(2,1)}, u32[]{:S(2)}) copy-start(bf16[192,1636]{1,0:T(8,128)(2,1)} %get-tuple-element.73) | copy-start | bytes 1884676
  88.4 7.4 %copy-start.25 = (bf16[64,1088]{0,1:T(8,128)(2,1)S(1)}, bf16[64,1088]{0,1:T(8,128)(2,1)}, u32[]{:S(2)}) copy-start(bf16[64,1088]{0,1:T(8,128)(2,1)} %get-tuple-element.30) | copy-start | bytes 417796
  88.4 7.4 %copy-start.26 = (bf16[64,1088]{0,1:T(8,128)(2,1)S(1)}, bf16[64,1088]{0,1:T(8,128)(2,1)}, u32[]{:S(2)}) copy-start(bf16[64,1088]{0,1:T(8,128)(2,1)} %get-tuple-element.31) | copy-start | bytes 417796
  88.4 7.4 %copy-start.27 = (bf16[64,1088]{0,1:T(8,128)(2,1)S(1)}, bf16[64,1088]{0,1:T(8,128)(2,1)}, u32[]{:S(2)}) copy-start(bf16[64,1088]{0,1:T(8,128)(2,1)} %get-tuple-element.49) | copy-start | bytes 417796
  88.4 7.4 %copy-start.28 = (bf16[64,1088]{0,1:T(8,128)(2,1)S(1)}, bf16[64,1088]{0,1:T(8,128)(2,1)}, u32[]{:S(2)}) copy-start(bf16[64,1088]{0,1:T(8,128)(2,1)} %get-tuple-element.50) | copy-start | bytes 417796
  88.4 7.4 %copy-start.29 = (bf16[64,1088]{0,1:T(8,128)(2,1)S(1)}, bf16[64,1088]{0,1:T(8,128)(2,1)}, u32[]{:S(2)}) copy-start(bf16[64,1088]{0,1:T(8,128)(2,1)} %get-tuple-element.51) | copy-start | bytes 417796
  98.5 2.0 %copy-start.21 = (bf16[64,1088]{0,1:T(8,128)(2,1)S(1)}, bf16[64,1088]{0,1:T(8,128)(2,1)}, u32[]{:S(2)}) copy-start(bf16[64,1088]{0,1:T(8,128)(2,1)} %get-tuple-element.40) | copy-start | bytes 417796
  98.5 2.0 %copy-start.22 = (bf16[64,1088]{0,1:T(8,128)(2,1)S(1)}, bf16[64,1088]{0,1:T(8,128)(2,1)}, u32[]{:S(2)}) copy-start(bf16[64,1088]{0,1:T(8,128)(2,1)} %get-tuple-element.41) | copy-start | bytes 417796
  98.5 2.0 %copy-start.23 = (bf16[64,1088]{0,1:T(8,128)(2,1)S(1)}, bf16[64,1088]{0,1:T(8,128)(2,1)}, u32[]{:S(2)}) copy-start(bf16[64,1088]{0,1:T(8,128)(2,1)} %get-tuple-element.42) | copy-start | bytes 417796
  98.5 2.0 %copy-start.24 = (bf16[64,1088]{0,1:T(8,128)(2,1)S(1)}, bf16[64,1088]{0,1:T(8,128)(2,1)}, u32[]{:S(2)}) copy-start(bf16[64,1088]{0,1:T(8,128)(2,1)} %get-tuple-element.43) | copy-start | bytes 417796
  103.2 2.6 %copy-start.16 = (bf16[64,1088]{0,1:T(8,128)(2,1)S(1)}, bf16[64,1088]{0,1:T(8,128)(2,1)}, u32[]{:S(2)}) copy-start(bf16[64,1088]{0,1:T(8,128)(2,1)} %get-tuple-element.29) | copy-start | bytes 417796
  103.2 2.6 %copy-start.17 = (bf16[64,1088]{0,1:T(8,128)(2,1)S(1)}, bf16[64,1088]{0,1:T(8,128)(2,1)}, u32[]{:S(2)}) copy-start(bf16[64,1088]{0,1:T(8,128)(2,1)} %get-tuple-element.32) | copy-start | bytes 417796
  103.2 2.6 %copy-start.18 = (bf16[64,1088]{0,1:T(8,128)(2,1)S(1)}, bf16[64,1088]{0,1:T(8,128)(2,1)}, u32[]{:S(2)}) copy-start(bf16[64,1088]{0,1:T(8,128)(2,1)} %get-tuple-element.33) | copy-start | bytes 417796
  103.2 2.6 %copy-start.19 = (bf16[64,1088]{0,1:T(8,128)(2,1)S(1)}, bf16[64,1088]{0,1:T(8,128)(2,1)}, u32[]{:S(2)}) copy-start(bf16[64,1088]{0,1:T(8,128)(2,1)} %get-tuple-element.34) | copy-start | bytes 417796
  103.2 2.6 %copy-start.20 = (bf16[64,1088]{0,1:T(8,128)(2,1)S(1)}, bf16[64,1088]{0,1:T(8,128)(2,1)}, u32[]{:S(2)}) copy-start(bf16[64,1088]{0,1:T(8,128)(2,1)} %get-tuple-element.35) | copy-start | bytes 417796
  171.0 2.8 %copy-start.1 = (bf16[9,192,64]{1,2,0:T(8,128)(2,1)S(1)}, bf16[9,192,64]{1,2,0:T(8,128)(2,1)}, u32[]{:S(2)}) copy-start(bf16[9,192,64]{1,2,0:T(8,128)(2,1)} %param.7) | copy-start | bytes 663556

commit v3 on v0

--- a/solution.py
+++ b/solution.py
@@ -47,7 +47,7 @@
     share = lax.dot_general(
         pre_grad, stack, (((1,), (1,)), ((), ())), preferred_element_type=jnp.float32
     )
-    return share.reshape(pre_grad.shape[0], taps, -1).transpose(1, 0, 2)
+    return share
 
 
 def gates(from_input, from_state, previous, channels):
@@ -76,7 +76,7 @@
     return (input_pre, state_pre, grad_state * update)
 
 
-def reduce_kernel(rows, cols, x_ref, out_ref, got_row, summed, got_col, reduced, gathered, send_sem, recv_sem, own_sem):
+def reduce_kernel(rows, cols, x_ref, out_ref, got_row, summed, got_col, reduced, send_sem, recv_sem, own_sem):
     mesh_ids = pl.DeviceIdType.MESH
     me_row, me_col = lax.axis_index("row"), lax.axis_index("col")
     barrier = pltpu.get_barrier_semaphore()
@@ -85,7 +85,7 @@
             peer = lax.rem(me + distance, count)
             pl.semaphore_signal(barrier, inc=1, device_id={axis: peer}, device_id_type=mesh_ids)
     pl.semaphore_wait(barrier, rows + cols - 2)
-    piece = summed.shape[0] // cols
+    chunk = summed.shape[0]
 
     def phase(index, axis, me, count, source, target):
         copies = []
@@ -107,51 +107,42 @@
         for copy in copies:
             copy.wait()
 
-    phase(0, "row", me_row, rows, lambda peer: x_ref.at[peer], got_row)
+    phase(0, "row", me_row, rows, lambda peer: x_ref.at[pl.ds(pl.multiple_of(peer * chunk, 8), chunk)], got_row)
     total = got_row[0]
     for index in range(1, rows):
         total = total + got_row[index]
     summed[...] = total
-    phase(
-        1, "col", me_col, cols,
-        lambda peer: summed.at[pl.ds(pl.multiple_of(peer * piece, piece), piece)], got_col,
-    )
+    phase(1, "col", me_col, cols, lambda peer: summed, got_col)
     total = got_col[0]
     for index in range(1, cols):
         total = total + got_col[index]
     reduced[...] = total
-    phase(2, "col", me_col, cols, lambda peer: reduced, gathered)
-    phase(3, "row", me_row, rows, lambda peer: gathered, out_ref)
+    phase(2, "row", me_row, rows, lambda peer: reduced, out_ref)
 
 
 def all_sum(parts):
-    both = jnp.stack(parts, 0)
+    both = jnp.concatenate(parts, 0)
     rows, cols = lax.axis_size("row"), lax.axis_size("col")
-    lanes = 128
-    piece = -(-both.size // (rows * cols * lanes))
-    piece = -(-piece // 8) * 8
-    chunk = cols * piece * lanes
-    padded_size = rows * chunk
-    flat = jnp.pad(both.reshape(-1), (0, padded_size - both.size))
+    chunk = both.shape[0] // rows
+    width = both.shape[1]
     count = max(rows, cols)
     out = pl.pallas_call(
         functools.partial(reduce_kernel, rows, cols),
-        out_shape=jax.ShapeDtypeStruct((rows, cols, piece, lanes), jnp.float32),
+        out_shape=jax.ShapeDtypeStruct((rows, chunk, width), jnp.float32),
         in_specs=[pl.BlockSpec(memory_space=pltpu.VMEM)],
         out_specs=pl.BlockSpec(memory_space=pltpu.VMEM),
         scratch_shapes=[
-            pltpu.VMEM((rows, cols * piece, lanes), jnp.float32),
-            pltpu.VMEM((cols * piece, lanes), jnp.float32),
-            pltpu.VMEM((cols, piece, lanes), jnp.float32),
-            pltpu.VMEM((piece, lanes), jnp.float32),
-            pltpu.VMEM((cols, piece, lanes), jnp.float32),
-            pltpu.SemaphoreType.DMA((4, count)),
-            pltpu.SemaphoreType.DMA((4, count)),
-            pltpu.SemaphoreType.DMA((4,)),
+            pltpu.VMEM((rows, chunk, width), jnp.float32),
+            pltpu.VMEM((chunk, width), jnp.float32),
+            pltpu.VMEM((cols, chunk, width), jnp.float32),
+            pltpu.VMEM((chunk, width), jnp.float32),
+            pltpu.SemaphoreType.DMA((3, count)),
+            pltpu.SemaphoreType.DMA((3, count)),
+            pltpu.SemaphoreType.DMA((3,)),
         ],
         compiler_params=pltpu.CompilerParams(collective_id=0, has_side_effects=True),
-    )(flat.reshape(rows, cols * piece, lanes))
-    return out.reshape(-1)[: both.size].reshape(both.shape)
+    )(both)
+    return jnp.split(out.reshape(both.shape), len(parts), 0)
 
 
 def local(frames, state, input_weight, state_weight, cotangent):
@@ -215,6 +206,10 @@
         weight_flat(p, f, offsets, margin, length) for p, f in zip(state_pres, state_fields)
     )
     input_sum, state_sum = all_sum([input_sum, state_sum])
+    taps, out_ch, in_ch = input_weight.shape
+    input_sum = input_sum.reshape(out_ch, taps, in_ch).transpose(1, 0, 2)
+    taps, out_ch, in_ch = state_weight.shape
+    state_sum = state_sum.reshape(out_ch, taps, in_ch).transpose(1, 0, 2)
     loss_scale = (rows * lax.axis_size("row") * cols * lax.axis_size("col")) ** (-0.5)
 
     def crop(flat):

time: 151 us -> 158 us (1.046)
  Pallas kernels: 55.5 us -> 69.8 us
  matrix products: 16.3 us -> 12.6 us
  local copies, waits for them, and re-layouts: 40.4 us -> 36.8 us
    pallas_call x1, Pallas kernels: 55.5 us -> 69.8 us  [all_sum(): pl.pallas_call(functools.partial(reduce_kernel, rows, cols), out_shape=ja...]
    add x2 -> x0, local copies, waits for them, and re-layouts: 3.3 us -> none  [the longest x1 2.06 us: local(): sum((weight_flat(p, f, offsets, margin, length) for p, f in zip(state_pre...]
    dot_general x4, matrix products: 8.85 us -> 6.08 us  [weight_flat(): lax.dot_general(pre_grad, stack, (((1,), (1,)), ((), ())), preferred_elem...]
    another operation x5 -> x4, other arithmetic: 4.44 us -> 2.21 us
    another operation x1 -> x0, local copies, waits for them, and re-layouts: 1.79 us -> none  [all_sum(): both = jnp.stack(parts, 0)]
    unnamed x108 -> x92, local copies, waits for them, and re-layouts: 14.2 us -> 14.4 us
  transfers between devices with their start and end apart: 4 -> 4, of which waited for: 2 -> 3; matrix products, arithmetic and copies ran while one was open for 2% -> 1% of each run, Pallas kernels for 0% -> 0%
where the time goes in v3:
time: 158 us; the launch traced here: 157 us
  Pallas kernels  69.8 us (44%)
  local copies, waits for them, and re-layouts  36.8 us (23%)
  other arithmetic  18.4 us (12%)
  matrix products  12.6 us (8%)
  starting transfers between devices  11.9 us (8%)
  waiting for transfers between devices  6.16 us (4%)
    pallas_call x1, Pallas kernels, all_sum(): pl.pallas_call(functools.partial(reduce_kernel, rows, cols), out_shape=ja...  69.8 us
    unnamed x92, local copies, waits for them, and re-layouts  14.4 us
    ppermute x2, starting transfers between devices, padded_2(): before = lax.ppermute(last, axis, up)  8.68 us
    concatenate x2, other arithmetic, padded_2(): array = jnp.concatenate([before, array, after], axis=dim)  7.86 us
    dot_general x4, matrix products, weight_flat(): lax.dot_general(pre_grad, stack, (((1,), (1,)), ((), ())), preferred_elem...  6.08 us
    reshape x2, local copies, waits for them, and re-layouts, crop(): flat.reshape(-1, ext_rows, ext_cols)[:, halo:halo + rows, halo:halo + cols]  4.58 us
    ppermute x2, waiting for transfers between devices, padded_2(): after = lax.ppermute(first, axis, down)  4.52 us
    dot_general x4, matrix products, conv_flat(): return jnp.dot(matrix, stack, preferred_element_type=jnp.float32)  3.53 us
  transfers between devices with their start and end apart: 4, of which 3 were waited for; matrix products, arithmetic and copies ran while one was open for 1% of the time, Pallas kernels for 0%

profile of v3, /device:TPU:1, one launch (start us, length us, event | category | flops | bytes accessed | tf_op | source)
XLA Modules:
  0.0 157.1 jit_solution(18093149238908617831)
XLA Ops:
  0.6 1.2 pad_maximum_fusion.9
  2.0 4.5 %collective-permute-start = (bf16[256,4,128]{2,1,0:T(4,128)(2,1)S(1)}, bf16[256,4,128]{2,1,0:T(4,128)(2,1)S(1)}, u32[]{:S(2)}, u32[]{:S(2)}) collective-permute-start(bf16[256,4,128]{2,1,0:T(4,128)(2,1)S(1)} %get-tuple-element.38), channel_id=1, source_target_pairs={{0,16},{16,32},{32,48},{48,64},{64,80},{80,96},{96,112},{112,128},... | collective-permute-start | bytes 786440 | tf_op jit(solution)/shard_map/ppermute | solution.py:20
  6.5 1.9 %collective-permute-start.1 = (bf16[256,4,128]{2,1,0:T(4,128)(2,1)S(1)}, bf16[256,4,128]{2,1,0:T(4,128)(2,1)S(1)}, u32[]{:S(2)}, u32[]{:S(2)}) collective-permute-start(bf16[256,4,128]{2,1,0:T(4,128)(2,1)S(1)} %get-tuple-element.39), channel_id=1, source_target_pairs={{16,0},{32,16},{48,32},{64,48},{80,64},{96,80},{112,96},{128,112},... | collective-permute-start | bytes 786440 | tf_op jit(solution)/shard_map/ppermute | solution.py:21
  8.6 1.2 collective-permute-done
  9.8 4.5 %collective-permute-done.1 = bf16[256,4,128]{2,1,0:T(4,128)(2,1)S(1)} collective-permute-done((bf16[256,4,128]{2,1,0:T(4,128)(2,1)S(1)}, bf16[256,4,128]{2,1,0:T(4,128)(2,1)S(1)}, u32[]{:S(2)}, u32[]{:S(2)}) %collective-permute-start.1) | collective-permute-done | bytes 262176 | tf_op jit(solution)/shard_map/ppermute | solution.py:21
  14.3 0.7 copy-done.18
  15.0 1.7 %pad_maximum_fusion.1 = bf16[256,16,128]{2,1,0:T(8,128)(2,1)S(1)} fusion(bf16[256,4,128]{2,1,0:T(4,128)(2,1)S(1)} %collective-permute-done.1, bf16[64,8,128]{2,1,0:T(8,128)(2,1)} %param.9, bf16[64,8,128]{2,1,0:T(8,128)(2,1)} %param.6, bf16[128,8,128]{2,1,0:T(8,128)(2,1)} %bitcast.50, bf16[256,4,128]{2,1,0:T(4,128)(2,1)S(1)} %collective-permute-done), kind=kLoop, calls=%fused_computation.11 | loop fusion | flops 5242880 | bytes 2097152 | tf_op jit(solution)/shard_map/concatenate | solution.py:22
  16.7 0.5 fusion.65
  17.2 1.5 copy.22
  18.8 0.9 copy.23
  19.7 1.3 collective-permute-start.3
  21.0 4.2 %collective-permute-start.2 = (bf16[256,16,4]{0,1,2:T(8,128)(2,1)}, bf16[256,16,4]{0,1,2:T(8,128)(2,1)S(1)}, u32[]{:S(2)}, u32[]{:S(2)}) collective-permute-start(bf16[256,16,4]{0,1,2:T(8,128)(2,1)} %copy.22), channel_id=1, source_target_pairs={{0,1},{1,2},{2,3},{3,4},{4,5},{5,6},{6,7},{7,8},{8,9},{9,10},{10,1... | collective-permute-start | bytes 98312 | tf_op jit(solution)/shard_map/ppermute | solution.py:20
  26.0 0.4 collective-permute-done.2
  26.5 1.0 copy.24
  27.5 1.0 copy.25
  28.6 6.2 %pad_maximum_fusion = bf16[256,16,136]{2,1,0:T(8,128)(2,1)S(1)} fusion(bf16[256,16,4]{2,1,0:T(8,128)(2,1)S(1)} %copy.25, bf16[256,4,128]{2,1,0:T(4,128)(2,1)} %copy-done.18, bf16[64,8,128]{2,1,0:T(8,128)(2,1)S(1)} %copy-done.15, bf16[64,8,128]{2,1,0:T(8,128)(2,1)S(1)} %copy-done.16, bf16[128,8,128]{2,1,0:T(8,128)(2,1)S(1)} %bitcast.51, ...), kind=kLoop, calls=%fused_computation.8 | loop fusion | flops 7798784 | bytes 2228224 | tf_op jit(solution)/shard_map/concatenate | solution.py:22
  34.8 1.2 fusion.64
  36.0 0.7 slice.269
  36.6 1.7 %slice.291 = bf16[64,2176]{1,0:T(8,128)(2,1)S(1)} reshape(bf16[64,16,136]{2,1,0:T(8,128)(2,1)} %get-tuple-element.31) | data formatting | bytes 557056 | tf_op jit(solution)/shard_map/slice | solution.py:162
  38.4 1.7 %slice.280 = bf16[64,2176]{1,0:T(8,128)(2,1)S(1)} reshape(bf16[64,16,136]{2,1,0:T(8,128)(2,1)} %get-tuple-element.32) | data formatting | bytes 557056 | tf_op jit(solution)/shard_map/slice | solution.py:160
  40.1 1.4 reshape.119
  44.2 0.9 convolution_bitcast_fusion.2
  45.0 0.4 copy-done.8
  45.4 0.9 convolution_bitcast_fusion.1
  46.3 1.4 fusion.47
  48.9 0.9 convolution_bitcast_fusion
  51.0 0.9 convolution_bitcast_fusion.3
  52.1 0.4 fusion.59
  52.6 0.8 fusion.46
  53.9 2.1 %fusion.6 = f32[192,576]{1,0:T(8,128)} fusion(bf16[576,2176]{1,0:T(8,128)(2,1)S(1)} %slice_dynamic-update-slice_fusion.16, pred[2176]{0:T(1024)(128)(4,1)S(1)} %and.82, bf16[64,2176]{1,0:T(8,128)(2,1)S(1)} %get-tuple-element.28, bf16[64,2176]{1,0:T(8,128)(2,1)S(1)} %get-tuple-element.27, bf16[64,2176]{1,0:T(8,128)(2,1)S(1)} %fusion.23), kind=kOutput, calls=%fused_computation.23 | convolution fusion | flops 484220928 | bytes 3786880 | tf_op jit(solution)/shard_map/dot_general | solution.py:47
  55.9 1.9 %fusion.2 = f32[192,576]{1,0:T(8,128)} fusion(bf16[576,2176]{1,0:T(8,128)(2,1)S(1)} %slice_dynamic-update-slice_fusion.40, bf16[64,2176]{1,0:T(8,128)(2,1)S(1)} %get-tuple-element.18, pred[2176]{0:T(1024)(128)(4,1)S(1)} %and.82, bf16[64,2176]{1,0:T(8,128)(2,1)S(1)} %get-tuple-element.27, bf16[64,2176]{1,0:T(8,128)(2,1)S(1)} %fusion.23), kind=kOutput, calls=%fused_computation.18 | convolution fusion | flops 484220928 | bytes 3786880 | tf_op jit(solution)/shard_map/dot_general | solution.py:47
  57.8 3.2 %reshape.116 = bf16[64,16,136]{2,1,0:T(8,128)(2,1)} reshape(bf16[64,2176]{1,0:T(8,128)(2,1)} %fusion.46) | data formatting | bytes 557056 | tf_op jit(solution)/shard_map/reshape | solution.py:216
  61.0 1.8 %slice.356 = bf16[64,8,128]{2,1,0:T(8,128)(2,1)} slice(bf16[64,16,136]{2,1,0:T(8,128)(2,1)} %reshape.116), slice={[0:64], [4:12], [4:132]} | slice | bytes 262144 | tf_op jit(solution)/shard_map/slice | solution.py:216
  66.1 1.5 fusion.58
  67.7 1.5 multiply_convert_fusion.1
  69.6 1.1 convolution_add_fusion
  70.7 0.6 copy-done.7
  71.4 1.1 convolution_add_fusion.1
  72.5 1.0 pad_maximum_fusion.2.x_ref
  73.5 69.8 %shard_map.84 = f32[16,24,576]{2,1,0:T(8,128)} custom-call(f32[384,576]{1,0:T(8,128)} %pad_maximum_fusion.2.x_ref), custom_call_target="tpu_custom_call" | custom-call | tf_op jit(solution)/shard_map/pallas_call | solution.py:129
  143.3 2.2 %slice_multiply_fusion = (f32[8,24,576]{2,1,0:T(8,128)}, f32[8,24,576]{2,1,0:T(8,128)}) fusion(f32[16,24,576]{2,1,0:T(8,128)} %shard_map.84), kind=kLoop, calls=%fused_computation.95 | loop fusion | flops 221184 | bytes 1769472 | tf_op jit(solution)/shard_map/mul | solution.py:218
  145.5 1.3 mul.142
  146.8 1.3 copy.28
  148.1 1.3 mul.139
  149.4 1.3 copy.27
  153.4 1.5 fusion
  154.9 1.4 reshape.118
  156.3 0.8 slice.358
  (109 shorter events, 13.1 us)
Async XLA Ops:
  0.6 43.3 %copy-start = (bf16[9,192,64]{1,2,0:T(8,128)(2,1)S(1)}, bf16[9,192,64]{1,2,0:T(8,128)(2,1)}, u32[]{:S(2)}) copy-start(bf16[9,192,64]{1,2,0:T(8,128)(2,1)} %param.7) | copy-start | bytes 663556
  2.0 7.8 %collective-permute-start = (bf16[256,4,128]{2,1,0:T(4,128)(2,1)S(1)}, bf16[256,4,128]{2,1,0:T(4,128)(2,1)S(1)}, u32[]{:S(2)}, u32[]{:S(2)}) collective-permute-start(bf16[256,4,128]{2,1,0:T(4,128)(2,1)S(1)} %get-tuple-element.38), channel_id=1, source_target_pairs={{0,16},{16,32},{32,48},{48,64},{64,80},{80,96},{96,112},{112,128},... | collective-permute-start | bytes 786440 | tf_op jit(solution)/shard_map/ppermute | solution.py:20
  6.5 7.8 %collective-permute-start.1 = (bf16[256,4,128]{2,1,0:T(4,128)(2,1)S(1)}, bf16[256,4,128]{2,1,0:T(4,128)(2,1)S(1)}, u32[]{:S(2)}, u32[]{:S(2)}) collective-permute-start(bf16[256,4,128]{2,1,0:T(4,128)(2,1)S(1)} %get-tuple-element.39), channel_id=1, source_target_pairs={{16,0},{32,16},{48,32},{64,48},{80,64},{96,80},{112,96},{128,112},... | collective-permute-start | bytes 786440 | tf_op jit(solution)/shard_map/ppermute | solution.py:21
  9.8 4.5 %copy-start.17 = (bf16[256,4,128]{2,1,0:T(4,128)(2,1)}, bf16[256,4,128]{2,1,0:T(4,128)(2,1)S(1)}, u32[]{:S(2)}) copy-start(bf16[256,4,128]{2,1,0:T(4,128)(2,1)S(1)} %collective-permute-done) | copy-start | bytes 786436
  14.3 0.7 copy-start.18
  16.7 8.8 %copy-start.12 = (bf16[9,192,64]{1,2,0:T(8,128)(2,1)S(1)}, bf16[9,192,64]{1,2,0:T(8,128)(2,1)}, u32[]{:S(2)}) copy-start(bf16[9,192,64]{1,2,0:T(8,128)(2,1)} %param.8) | copy-start | bytes 663556
  18.8 9.8 %copy-start.13 = (bf16[2,64,8,128]{3,2,1,0:T(8,128)(2,1)S(1)}, bf16[2,64,8,128]{3,2,1,0:T(8,128)(2,1)}, u32[]{:S(2)}) copy-start(bf16[2,64,8,128]{3,2,1,0:T(8,128)(2,1)} %param.5) | copy-start | bytes 786436
  18.8 9.8 %copy-start.15 = (bf16[64,8,128]{2,1,0:T(8,128)(2,1)S(1)}, bf16[64,8,128]{2,1,0:T(8,128)(2,1)}, u32[]{:S(2)}) copy-start(bf16[64,8,128]{2,1,0:T(8,128)(2,1)} %param.9) | copy-start | bytes 393220
  18.8 9.8 %copy-start.16 = (bf16[64,8,128]{2,1,0:T(8,128)(2,1)S(1)}, bf16[64,8,128]{2,1,0:T(8,128)(2,1)}, u32[]{:S(2)}) copy-start(bf16[64,8,128]{2,1,0:T(8,128)(2,1)} %param.6) | copy-start | bytes 393220
  19.7 7.8 %collective-permute-start.3 = (bf16[256,16,4]{0,1,2:T(8,128)(2,1)S(1)}, bf16[256,16,4]{0,1,2:T(8,128)(2,1)S(1)}, u32[]{:S(2)}, u32[]{:S(2)}) collective-permute-start(bf16[256,16,4]{0,1,2:T(8,128)(2,1)S(1)} %copy.23), channel_id=1, source_target_pairs={{1,0},{2,1},{3,2},{4,3},{5,4},{6,5},{7,6},{8,7},{9,8},{10,9},{11,1... | collective-permute-start | bytes 98312 | tf_op jit(solution)/shard_map/ppermute | solution.py:21
  21.0 5.5 %collective-permute-start.2 = (bf16[256,16,4]{0,1,2:T(8,128)(2,1)}, bf16[256,16,4]{0,1,2:T(8,128)(2,1)S(1)}, u32[]{:S(2)}, u32[]{:S(2)}) collective-permute-start(bf16[256,16,4]{0,1,2:T(8,128)(2,1)} %copy.22), channel_id=1, source_target_pairs={{0,1},{1,2},{2,3},{3,4},{4,5},{5,6},{6,7},{7,8},{8,9},{9,10},{10,1... | collective-permute-start | bytes 98312 | tf_op jit(solution)/shard_map/ppermute | solution.py:20
  42.7 1.5 copy-start.6
  43.9 1.5 copy-start.8
  45.0 1.3 copy-start.1
  51.0 1.1 copy-start.2
  52.5 1.2 copy-start.4
  64.6 1.1 copy-start.3
  64.6 1.2 copy-start.5
  64.6 1.4 copy-start.10
  64.6 1.5 copy-start.14
  67.7 1.9 %copy-start.9 = (bf16[576,2176]{1,0:T(8,128)(2,1)S(1)}, bf16[576,2176]{1,0:T(8,128)(2,1)}, u32[]{:S(2)}) copy-start(bf16[576,2176]{1,0:T(8,128)(2,1)} %copy-done.8) | copy-start | bytes 7520260
  67.7 1.9 %copy-start.20 = (f32[192,576]{1,0:T(8,128)S(1)}, f32[192,576]{1,0:T(8,128)}, u32[]{:S(2)}) copy-start(f32[192,576]{1,0:T(8,128)} %fusion.6) | copy-start | bytes 1327108
  69.6 1.7 %copy-start.7 = (bf16[576,2176]{1,0:T(8,128)(2,1)S(1)}, bf16[576,2176]{1,0:T(8,128)(2,1)}, u32[]{:S(2)}) copy-start(bf16[576,2176]{1,0:T(8,128)(2,1)} %copy-done.6) | copy-start | bytes 7520260
  69.6 1.8 %copy-start.19 = (f32[192,576]{1,0:T(8,128)S(1)}, f32[192,576]{1,0:T(8,128)}, u32[]{:S(2)}) copy-start(f32[192,576]{1,0:T(8,128)} %fusion.2) | copy-start | bytes 1327108
  152.4 1.1 copy-start.11
